TPU v7x, 256 devices: a whole 4x4x8 slice. The times are simulated.
256 devices in a mesh: scan: 8 (over x, core), obj: 32 (over y, z).
Axes of the slice: x: 4, y: 4, z: 8, core: 2. Of those that a mesh axis runs over, the one named last changes fastest.
Arguments:
- object_slices: float32 [2, 2, 8192, 2048], P(None, None, 'obj'), may hold values from -4 to 4
- probe: float32 [2, 2, 256, 256], replicated, may hold values from -6 to 6
- measured: bfloat16 [8, 32, 2, 256, 256], P('scan', 'obj'), may hold values from 0 to 4
- positions: int32 [8, 32, 2, 2], P('scan', 'obj'), may hold values from 0 to 1792, as said below
- counts: int32 [8, 32], P('scan', 'obj'), may hold values from 0 to 2, as said below
Outputs:
- object_grad: float32 [2, 2, 8192, 2048], P(None, None, 'obj', 'scan')
- probe_grad: float32 [2, 2, 256, 256], P(None, None, 'obj', 'scan')
Inputs may be any that keep to these rules, and one draw needn't show every extreme that they name: In every tile o the counts over the 8 batches sum to exactly 8, and some batch of every tile has 2 live patterns. `positions`: the row offset is below 256, the column at most 1792.
All inputs are finite; a program needn't handle non-finite values.
Results may differ from a plain program's by a relative error of at most 0.013.
Values may be sent and summed in bfloat16 or wider, within the bound.
A program may use at most 128 MiB of HBM per device.

v0:
```python
import math

import jax
import jax.numpy as jnp
from jax import lax
from jax.sharding import PartitionSpec as P


def shifted(block, axis, distance):
    devices = range(lax.axis_size(axis))
    route = [((i - distance) % len(devices), i) for i in devices]
    return lax.ppermute(block, axis, route)


def dft_matrix(length, sign):
    index_row = jnp.arange(length, dtype=jnp.int32)
    product = index_row[:, None] * index_row[None, :] % length
    angles = product.astype(jnp.float32) * (2.0 * math.pi / length)
    factor = 1.0 / math.sqrt(length)
    real_part = jnp.cos(angles) * factor
    imag_part = sign * jnp.sin(angles) * factor
    stacked = jnp.stack([jnp.stack([real_part, -imag_part]), jnp.stack([imag_part, real_part])])
    return stacked.astype(jnp.bfloat16)


def fresnel_kernel(length):
    index_row = jnp.arange(length, dtype=jnp.int32)
    freqs = jnp.where(index_row < length // 2, index_row, index_row - length)
    squares = freqs * freqs
    summed = (squares[:, None] + squares[None, :]) % (4 * length)
    phases = summed.astype(jnp.float32) * (2.0 * math.pi / (4 * length))
    return jnp.stack([jnp.cos(phases), -jnp.sin(phases)])


def transform(field_in, matrix):
    partial_out = jnp.einsum(
        "pqab,qbc->pac", matrix, field_in.astype(jnp.bfloat16), preferred_element_type=jnp.float32
    )
    return jnp.einsum(
        "qab,pqbc->pac",
        partial_out.astype(jnp.bfloat16),
        matrix,
        preferred_element_type=jnp.float32,
    )


def complex_mul(first_op, second_op):
    return jnp.stack(
        [
            first_op[0] * second_op[0] - first_op[1] * second_op[1],
            first_op[0] * second_op[1] + first_op[1] * second_op[0],
        ]
    )


def conj_mul(first_op, second_op):
    return jnp.stack(
        [
            first_op[0] * second_op[0] + first_op[1] * second_op[1],
            first_op[0] * second_op[1] - first_op[1] * second_op[0],
        ]
    )


def pattern_terms(patches, probe, pattern_data, weight, forward, inverse, kernel):
    layers = patches.shape[0]

    def forward_mode(mode_probe):
        arrivals = [mode_probe]
        field_now = complex_mul(mode_probe, patches[0])
        spectrum = transform(field_now, forward)
        field_now = transform(complex_mul(kernel, spectrum), inverse)
        arrivals.append(field_now)
        field_now = complex_mul(field_now, patches[1])
        return (transform(field_now, forward), jnp.stack(arrivals))

    far_field, arrivals = jax.vmap(forward_mode)(probe)
    intensity = jnp.sum(far_field[:, 0] ** 2 + far_field[:, 1] ** 2, axis=0)
    misfit = (intensity - pattern_data.astype(jnp.float32)) * weight

    def back_mode(mode_far, mode_arrivals):
        adjoint = transform(misfit[None] * mode_far, inverse)
        layer_grads = [None] * layers
        for layer_idx in reversed(range(layers)):
            layer_grads[layer_idx] = conj_mul(mode_arrivals[layer_idx], adjoint)
            adjoint = conj_mul(patches[layer_idx], adjoint)
            if layer_idx > 0:
                spectrum = transform(adjoint, forward)
                adjoint = transform(conj_mul(kernel, spectrum), inverse)
        return (jnp.stack(layer_grads), adjoint)

    patch_grads, probe_grads = jax.vmap(back_mode)(far_field, arrivals)
    return (jnp.sum(patch_grads, axis=0), probe_grads)


def body(object_slices, probe, measured, positions, counts):
    layers = object_slices.shape[0]
    tile_rows = object_slices.shape[2]
    tile_cols = object_slices.shape[3]
    length = probe.shape[-1]
    slots_all = measured.shape[2]
    forward = dft_matrix(length, -1.0)
    inverse = dft_matrix(length, 1.0)
    kernel = fresnel_kernel(length)
    zero_index = jnp.zeros((), jnp.int32)
    slot_data = measured[0, 0]
    slot_pos = positions[0, 0]
    slot_weight = (jnp.arange(slots_all, dtype=jnp.int32) < counts[0, 0]).astype(jnp.float32)
    below = shifted(object_slices, "obj", -1)
    extended = jnp.concatenate([object_slices, below], axis=2)

    def cut_window(pattern_pos):
        corner = (zero_index, zero_index, pattern_pos[0], pattern_pos[1])
        return lax.dynamic_slice(extended, corner, (layers, 2, length, length))

    slot_patches = jax.vmap(cut_window)(slot_pos)

    def slot_step(probe_sum, inputs):
        pattern_data, weight, patches = inputs
        patch_grad, probe_grad = pattern_terms(
            patches, probe, pattern_data, weight, forward, inverse, kernel
        )
        return (probe_sum + probe_grad, patch_grad)

    probe_zero = jnp.zeros(probe.shape, jnp.float32)
    probe_sum, slot_grads = lax.scan(slot_step, probe_zero, (slot_data, slot_weight, slot_patches))

    def add_window(band, inputs):
        patch_grad, pattern_pos = inputs
        corner = (zero_index, zero_index, pattern_pos[0], pattern_pos[1])
        current = lax.dynamic_slice(band, corner, (layers, 2, length, length))
        return (lax.dynamic_update_slice(band, current + patch_grad, corner), None)

    band_start = jnp.zeros((layers, 2, tile_rows + length, tile_cols), jnp.float32)
    band, leftover = lax.scan(add_window, band_start, (slot_grads, slot_pos))
    rim_back = shifted(band[:, :, tile_rows:], "obj", 1)
    tile_grad = band[:, :, :tile_rows].at[:, :, :length].add(rim_back)
    object_grad = lax.psum_scatter(tile_grad, "scan", scatter_dimension=3, tiled=True)
    live_total = lax.axis_size("scan") * lax.axis_size("obj") * slots_all // 2
    factor = 1.0 / math.sqrt(live_total)
    partial_probe = lax.psum_scatter(probe_sum, "obj", scatter_dimension=2, tiled=True)
    probe_total = lax.psum_scatter(partial_probe, "scan", scatter_dimension=3, tiled=True)
    return (object_grad, probe_total * factor)


def solution(mesh):
    return jax.shard_map(
        body,
        mesh=mesh,
        in_specs=(
            P(None, None, "obj", None),
            P(),
            P("scan", "obj", None, None, None),
            P("scan", "obj", None, None),
            P("scan", "obj"),
        ),
        out_specs=(P(None, None, "obj", "scan"), P(None, None, "obj", "scan")),
        check_vma=False,
    )
```

profile of v0, /device:TPU:1, one launch (start us, length us, event | category | flops | bytes accessed | tf_op | source)
XLA Modules:
  0.0 731.0 jit_solution(14991481800169718642)
XLA Ops:
  7.2 8.9 %collective-permute-start = (f32[2,2,256,2048]{3,2,1,0:T(8,128)}, f32[2,2,256,2048]{3,2,1,0:T(8,128)}, u32[]{:S(2)}, u32[]{:S(2)}) collective-permute-start(f32[2,2,256,2048]{3,2,1,0:T(8,128)} %param.13), channel_id=1, source_target_pairs={{1,0},{2,1},{3,2},{4,3},{5,4},{6,5},{7,6},{8,7},{9,8},{10,9},{11,1... | collective-permute-start | bytes 25165832 | tf_op jit(solution)/shard_map/ppermute | solution.py:12
  24.3 171.3 %collective-permute-done = f32[2,2,256,2048]{3,2,1,0:T(8,128)} collective-permute-done((f32[2,2,256,2048]{3,2,1,0:T(8,128)}, f32[2,2,256,2048]{3,2,1,0:T(8,128)}, u32[]{:S(2)}, u32[]{:S(2)}) %collective-permute-start) | collective-permute-done | bytes 8388640 | tf_op jit(solution)/shard_map/ppermute | solution.py:12
  195.6 11.7 %pad_maximum_fusion = f32[2,2,512,2048]{3,2,1,0:T(8,128)} fusion(f32[2,2,256,2048]{3,2,1,0:T(8,128)} %collective-permute-done, f32[2,2,256,2048]{3,2,1,0:T(8,128)} %param.13), kind=kLoop, calls=%fused_computation.118 | loop fusion | flops 4194304 | bytes 33554432 | tf_op jit(solution)/shard_map/concatenate | solution.py:110
  208.8 9.5 %while.30 = (s32[]{:T(128)}, f32[2,2,512,2048]{3,2,1,0:T(8,128)}, s32[2,4]{1,0:T(2,128)S(1)}, f32[2,2,2,256,256]{4,3,2,1,0:T(8,128)}, s32[]{:T(128)}) while((s32[]{:T(128)}, f32[2,2,512,2048]{3,2,1,0:T(8,128)}, s32[2,4]{1,0:T(2,128)S(1)}, f32[2,2,2,256,256]{4,3,2,1,0:T(8,128)}, s32[]{:T(128)}) %tuple.117), condition=%wide.while_cond.1, body=%wide.while_body.1.sunk | while | flops 2 | bytes 2098301 | solution.py:114
  209.5 4.1 bitcast_dynamic-update-slice_fusion.4
  214.2 4.1 bitcast_dynamic-update-slice_fusion.4
  219.8 71.4 %while.31 = (s32[]{:T(128)}, f32[2,2,256,256]{3,2,0,1:T(8,128)}, f32[2,2,2,256,256]{4,3,2,1,0:T(8,128)}, f32[2,2,2,256,256]{4,3,2,1,0:T(8,128)}, f32[2,2,256,256...) while((s32[]{:T(128)}, f32[2,2,256,256]{3,2,0,1:T(8,128)}, ...), condition=%wide.region_3.4_spmd.clone.clone.clone.clone, body=%wide.region_0.3_spmd.clone.clone.clone.clone.sunk | while | flops 3236495360 | bytes 113903368 | solution.py:126
  221.6 2.2 dynamic-slice_bitcast_fusion.5
  224.0 3.0 convolution_bitcast_fusion.16
  226.9 2.2 subtract_convert_fusion.6
  231.9 2.0 convolution_bitcast_fusion.17
  235.3 2.1 convolution_bitcast_fusion.18
  241.3 3.2 convolution_bitcast_fusion.19
  244.5 2.1 add_convert_fusion.5
  246.6 2.8 convolution_bitcast_fusion.20
  257.4 2.2 dynamic-slice_bitcast_fusion.5
  259.7 2.9 convolution_bitcast_fusion.16
  262.6 2.2 subtract_convert_fusion.6
  267.6 2.0 convolution_bitcast_fusion.17
  271.0 2.1 convolution_bitcast_fusion.18
  277.0 3.2 convolution_bitcast_fusion.19
  280.2 2.1 add_convert_fusion.5
  282.3 2.8 convolution_bitcast_fusion.20
  291.3 7.9 %broadcast_in_dim.9 = f32[2,2,512,2048]{3,2,1,0:T(8,128)} broadcast(f32[]{:T(128)} %constant.103.clone.1), dimensions={} | broadcast | bytes 16777220 | tf_op jit(solution)/shard_map/broadcast_in_dim | solution.py:134
  299.2 37.0 %while.29 = (s32[]{:T(128)}, f32[2,2,512,2048]{3,2,1,0:T(8,128)}, s32[2,2]{1,0:T(2,128)S(1)}, f32[2,2,2,256,256]{4,3,2,1,0:T(8,128)S(1)}, s32[]{:T(128)}, /*index=5*/s32[]{:T(128)}, s32[]{:T(128)}, s32[]{:T(128)}) while((s32[]{:T(128)}, f32[2,2,512,2048]{3,2,1,0:T(8,128)}, s32[2,2]{1,0:T(2,128)S(1)}, f32[2,2,2,256,256]{4,3,2,1,0:T(8,128)S(1)}, ...), condition=%wide.region_5.6_spmd, body=%wide.region_4.5_spmd.sunk | while | flops 262152 | bytes 5243093 | solution.py:135
  305.5 12.3 %dynamic_update_slice.14 = f32[2,2,512,2048]{3,2,1,0:T(8,128)} dynamic-update-slice(f32[2,2,512,2048]{3,2,1,0:T(8,128)} %get-tuple-element.589, f32[2,2,256,256]{3,2,1,0:T(8,128)S(1)} %bitcast_add_fusion.2, s32[]{:T(128)} %constant.102.clone.1..sunk, s32[]{:T(128)} %constant.102.clone.1..sunk, s32[]{:T(128)S(6)} %select_n.168, s32[]{:T(128)S(6)} %select_n.169) | dynamic-update-slice | bytes 2097156 | tf_op jit(solution)/shard_map/while/body/eval_jaxpr/dynamic_update_slice | solution.py:132
  324.2 11.9 %dynamic_update_slice.14 = f32[2,2,512,2048]{3,2,1,0:T(8,128)} dynamic-update-slice(f32[2,2,512,2048]{3,2,1,0:T(8,128)} %get-tuple-element.589, f32[2,2,256,256]{3,2,1,0:T(8,128)S(1)} %bitcast_add_fusion.2, s32[]{:T(128)} %constant.102.clone.1..sunk, s32[]{:T(128)} %constant.102.clone.1..sunk, s32[]{:T(128)S(6)} %select_n.168, s32[]{:T(128)S(6)} %select_n.169) | dynamic-update-slice | bytes 2097156 | tf_op jit(solution)/shard_map/while/body/eval_jaxpr/dynamic_update_slice | solution.py:132
  336.1 7.8 %slice.169 = f32[2,2,256,2048]{3,2,1,0:T(8,128)} slice(f32[2,2,512,2048]{3,2,1,0:T(8,128)} %get-tuple-element.121), slice={[0:2], [0:2], [256:512], [0:2048]} | slice | bytes 16777216 | tf_op jit(solution)/shard_map/slice | solution.py:136
  345.0 283.6 %reduce-scatter.8.cloned.1.call-done = f32[2,2,8,256]{3,2,1,0:T(8,128)} async-done(((f32[2,2,256,256]{3,2,1,0:T(8,128)}), f32[2,2,8,256]{3,2,1,0:T(8,128)}) %reduce-scatter.8.cloned.1.call-update) | async-done | bytes 32784 | tf_op jit(solution)/shard_map/reduce_scatter | solution.py:141
  630.8 11.7 %slice_add_fusion = f32[2,2,256,2048]{3,2,1,0:T(8,128)} fusion(f32[2,2,256,2048]{3,2,1,0:T(8,128)} %collective-permute-done.1, f32[2,2,512,2048]{3,2,1,0:T(8,128)} %get-tuple-element.121), kind=kLoop, calls=%fused_computation.119 | loop fusion | flops 2097152 | bytes 25165824 | tf_op jit(solution)/shard_map/add | solution.py:137
  642.6 23.3 %reduce-scatter.10.cloned.1.call-done = f32[32,32]{1,0:T(8,128)} async-done(((f32[256,32]{1,0:T(8,128)}), f32[32,32]{1,0:T(8,128)}) %reduce-scatter.10.cloned.1.call-update) | async-done | bytes 4112
  667.4 57.1 %reduce-scatter.6.cloned.1.call-done = f32[2,2,256,256]{3,2,1,0:T(8,128)} async-done(((f32[2,2,256,2048]{3,2,1,0:T(8,128)}), f32[2,2,256,256]{3,2,1,0:T(8,128)}) %reduce-scatter.6.cloned.1.call-update) | async-done | bytes 1048592 | tf_op jit(solution)/shard_map/reduce_scatter | solution.py:138
  (165 shorter events, 53.9 us)
Async XLA Ops:
  7.2 621.4 %reduce-scatter.8.cloned.1.call-start = ((), (), s32[]{:S(2)}) async-start(), calls=%async_computation.4 | async-start | bytes 1081344 | tf_op jit(solution)/shard_map/reduce_scatter | solution.py:141
  7.2 188.4 %collective-permute-start = (f32[2,2,256,2048]{3,2,1,0:T(8,128)}, f32[2,2,256,2048]{3,2,1,0:T(8,128)}, u32[]{:S(2)}, u32[]{:S(2)}) collective-permute-start(f32[2,2,256,2048]{3,2,1,0:T(8,128)} %param.13), channel_id=1, source_target_pairs={{1,0},{2,1},{3,2},{4,3},{5,4},{6,5},{7,6},{8,7},{9,8},{10,9},{11,1... | collective-permute-start | bytes 25165832 | tf_op jit(solution)/shard_map/ppermute | solution.py:12
  20.1 4.0 copy-start.23
  219.8 9.3 %copy-start.2 = (bf16[2,2,256,256]{3,2,1,0:T(8,128)(2,1)}, bf16[2,2,256,256]{3,2,1,0:T(8,128)(2,1)S(1)}, u32[]{:S(2)}) copy-start(bf16[2,2,256,256]{3,2,1,0:T(8,128)(2,1)S(1)} %get-tuple-element.573) | copy-start | bytes 1572868 | tf_op jit(solution)/shard_map/while
  221.6 5.3 copy-start.10
  221.6 5.3 copy-start.12
  223.8 3.1 copy-start.4
  223.8 7.1 copy-start.6
  229.1 1.8 copy-start.8
  231.9 2.1 copy-start.22
  241.3 3.2 copy-start.11
  241.3 3.2 copy-start.13
  241.3 5.3 copy-start.3
  246.6 2.8 copy-start.5
  252.1 2.1 copy-start.17
  255.5 9.2 %copy-start.2 = (bf16[2,2,256,256]{3,2,1,0:T(8,128)(2,1)}, bf16[2,2,256,256]{3,2,1,0:T(8,128)(2,1)S(1)}, u32[]{:S(2)}) copy-start(bf16[2,2,256,256]{3,2,1,0:T(8,128)(2,1)S(1)} %get-tuple-element.573) | copy-start | bytes 1572868 | tf_op jit(solution)/shard_map/while
  257.3 5.3 copy-start.10
  257.3 5.3 copy-start.12
  259.5 3.1 copy-start.4
  259.5 7.1 copy-start.6
  264.8 1.8 copy-start.8
  267.6 2.1 copy-start.22
  277.0 3.2 copy-start.11
  277.0 3.2 copy-start.13
  277.0 5.3 copy-start.3
  282.3 2.8 copy-start.5
  287.8 2.1 copy-start.17
  291.3 7.9 %copy-start.21 = (f32[2,2,2,256,256]{4,3,2,1,0:T(8,128)S(1)}, f32[2,2,2,256,256]{4,3,2,1,0:T(8,128)}, u32[]{:S(2)}) copy-start(f32[2,2,2,256,256]{4,3,2,1,0:T(8,128)} %get-tuple-element.583) | copy-start | bytes 6291460
  336.1 7.8 %copy-start.18 = (f32[2,2,256,256]{3,2,0,1:T(8,128)S(1)}, f32[2,2,256,256]{3,2,0,1:T(8,128)}, u32[]{:S(2)}) copy-start(f32[2,2,256,256]{3,2,0,1:T(8,128)} %get-tuple-element.122) | copy-start | bytes 3145732
  343.9 286.9 %collective-permute-start.1 = (f32[2,2,256,2048]{3,2,1,0:T(8,128)}, f32[2,2,256,2048]{3,2,1,0:T(8,128)}, u32[]{:S(2)}, u32[]{:S(2)}) collective-permute-start(f32[2,2,256,2048]{3,2,1,0:T(8,128)} %slice.169), channel_id=1, source_target_pairs={{31,0},{0,1},{1,2},{2,3},{3,4},{4,5},{5,6},{6,7},{7,8},{8,9},{9,10... | collective-permute-start | bytes 25165832 | tf_op jit(solution)/shard_map/ppermute | solution.py:12
  345.0 320.8 %reduce-scatter.10.cloned.1.call-start = ((), (), s32[]{:S(2)}) async-start(), calls=%async_computation.5 | async-start | bytes 147456
  630.8 93.7 %reduce-scatter.6.cloned.1.call-start = ((), (), s32[]{:S(2)}) async-start(), calls=%async_computation.3 | async-start | bytes 9437184 | tf_op jit(solution)/shard_map/reduce_scatter | solution.py:138
  (18 other events, 22.3 us)
Sparse Core Ops, SparseCore 0:
  345.1 283.4 reduce-scatter.7
  631.1 34.6 reduce-scatter.9
  669.0 55.4 reduce-scatter.5
where the time goes:
time: 733 us; the launch traced here: 731 us
  waiting for transfers between devices  535 us (73%)
  local copies, waits for them, and re-layouts  79.2 us (11%)
  other arithmetic  55.3 us (8%)
  matrix products  29.5 us (4%)
  between operations  14.5 us (2%)
  starting transfers between devices  9.05 us (1%)
  loops' own time  8.3 us (1%)
    reduce_scatter x1, waiting for transfers between devices, body(): lax.psum_scatter(probe_sum, 'obj', scatter_dimension=2, tiled=True)  284 us
    ppermute x2, waiting for transfers between devices, shifted(): return lax.ppermute(block, axis, route)  171 us
    reduce_scatter x1, waiting for transfers between devices, body(): lax.psum_scatter(tile_grad, 'scan', scatter_dimension=3, tiled=True)  57.1 us
    dot_general x12, matrix products, transform(): jnp.einsum('qab,pqbc->pac', partial_out.astype(jnp.bfloat16), matrix, pre...  29.5 us
    dynamic_update_slice x2, local copies, waits for them, and re-layouts, add_window(): return (lax.dynamic_update_slice(band, current + patch_grad, corner), None)  24.2 us
    unnamed x4, waiting for transfers between devices  23.3 us
  transfers between devices with their start and end apart: 5, of which 4 were waited for; matrix products, arithmetic and copies ran while one was open for 3% of the time, Pallas kernels for 0%

commit v1 on v0

v1 whole, which is shorter than its diff:
```python
import functools
import math

import jax
import jax.numpy as jnp
import numpy as np
from jax import lax
from jax.experimental import pallas as pl
from jax.experimental.pallas import tpu as pltpu
from jax.sharding import PartitionSpec as P

MESH = pl.DeviceIdType.MESH
BF = jnp.bfloat16
F32 = jnp.float32
N = 256
NS, NX, NO, NY, NZ = 8, 4, 32, 4, 8


def rem(a, b):
    return lax.rem(a, jnp.int32(b))


def tables():
    index = np.arange(N)
    angle = (np.outer(index, index) % N) * (2.0 * np.pi / N)
    rounded = lambda a: a.astype(np.float32).astype(BF)
    f_re, f_im = rounded(np.cos(angle) / 16.0), rounded(-np.sin(angle) / 16.0)
    fwd = f_re.astype(np.float64) + 1j * f_im.astype(np.float64)
    freq = np.where(index < N // 2, index, index - N)
    phase = np.exp(-2j * np.pi * ((freq * freq) % (4 * N)) / (4 * N))
    prop = np.conj(fwd) @ (phase[:, None] * fwd)
    return np.stack([f_re, f_im, rounded(prop.real), rounded(prop.imag)])


def remote(src, dst, send, recv, device):
    return pltpu.make_async_remote_copy(
        src_ref=src, dst_ref=dst, send_sem=send, recv_sem=recv, device_id=device, device_id_type=MESH
    )


def table_kernel(pos_ref, count_ref, out_ref, row_ref, tab_ref, send, recv):
    s, o = lax.axis_index("scan"), lax.axis_index("obj")
    up, down = rem(o + 1, NO), rem(o + NO - 1, NO)
    barrier = pltpu.get_barrier_semaphore()
    for k in range(NS):
        if k:
            pl.semaphore_signal(barrier, inc=1, device_id=(rem(s + k, NS), o), device_id_type=MESH)
        pl.semaphore_signal(barrier, inc=1, device_id=(rem(s + k, NS), down), device_id_type=MESH)
    lane = lax.broadcasted_iota(jnp.int32, (1, 128), 1)
    row = jnp.zeros((1, 128), jnp.int32)
    for j, value in enumerate((pos_ref[0, 0], pos_ref[0, 1], pos_ref[1, 0], pos_ref[1, 1], count_ref[0, 0])):
        row = jnp.where(lane == j, value, row)
    row_ref[...] = row
    tab_ref[s] = row
    pl.semaphore_wait(barrier, 2 * NS - 1)
    copies = []
    for k in range(NS):
        peer = rem(s + k, NS)
        source = rem(s + NS - k, NS)
        if k:
            copy = remote(row_ref, tab_ref.at[s], send.at[k], recv.at[k], (peer, o))
            copy.start()
            copies.append((copy, remote(row_ref, tab_ref.at[source], send.at[k], recv.at[k], (peer, o))))
        copy = remote(row_ref, tab_ref.at[NS + s], send.at[NS + k], recv.at[NS + k], (peer, up))
        copy.start()
        copies.append((copy, remote(row_ref, tab_ref.at[NS + source], send.at[NS + k], recv.at[NS + k], (peer, up))))
    for sent, landed in copies:
        sent.wait_send()
        landed.wait_recv()
    out_ref[...] = tab_ref[...]


def main_kernel(
    tab, tile_hbm, probe_hbm, meas_hbm, table_hbm, out_ref, pout_ref,
    tile_0, tile_1, probe, meas, tabs, e_f, e_i, e_h, e_c, hsend, hrecv, local, pattern, win, v, u, arr, far, cur,
    gsend, wins, acc, tsend, trecv, bsend, brecv, esend, erecv, ysend, yrecv, zsend, zrecv, xsend, xrecv,
    dma, send, recv,
):
    s, o = lax.axis_index("scan"), lax.axis_index("obj")
    x, core = lax.div(s, jnp.int32(2)), rem(s, 2)
    y, z = lax.div(o, jnp.int32(NZ)), rem(o, NZ)
    other = 1 - core
    partner = 2 * x + other
    right = [2 * rem(x + 1, NX) + c for c in range(2)]
    left = [2 * rem(x + 3, NX) + c for c in range(2)]
    right_me, left_me = 2 * rem(x + 1, NX) + core, 2 * rem(x + 3, NX) + core
    far_me, left_ot, right_ot, far_ot = (
        2 * rem(x + 2, NX) + core, 2 * rem(x + 3, NX) + other, 2 * rem(x + 1, NX) + other, 2 * rem(x + 2, NX) + other
    )
    far_at = [2 * rem(x + 2, NX) + c for c in range(2)]
    up, down = rem(o + 1, NO), rem(o + NO - 1, NO)
    tile = (tile_0, tile_1)
    sends = []

    loads = [
        pltpu.make_async_copy(table_hbm, tabs, dma.at[0]),
        pltpu.make_async_copy(probe_hbm, probe, dma.at[1]),
        pltpu.make_async_copy(meas_hbm, meas.at[pl.ds(2 * s, 2)], dma.at[2]),
    ]
    for layer in range(2):
        for b in range(NS):
            block = tile_hbm.at[layer, :, :, pl.ds(b * N, N)]
            loads.append(pltpu.make_async_copy(block, tile[layer].at[b], dma.at[3 + NS * layer + b]))
    for load in loads:
        load.start()

    barrier = pltpu.get_barrier_semaphore()
    peers = [(rem(s + k, NS), o) for k in range(1, NS)]
    peers += [(s, up), (s, down), (partner, down)]
    peers += [(s, rem(y + k, NY) * NZ + z) for k in range(1, NY)]
    peers += [(s, y * NZ + rem(z + k, NZ)) for k in range(1, NZ)]
    for peer in peers:
        pl.semaphore_signal(barrier, inc=1, device_id=peer, device_id_type=MESH)

    def assigned(base, n):
        start, found = jnp.int32(0), [jnp.int32(0)] * 3
        for t in range(NS):
            count = tab[base + t, 0, 4]
            for k in range(2):
                hit = (k < count) & (start + k == n)
                for j, value in enumerate((jnp.int32(2 * t + k), tab[base + t, 0, 2 * k], tab[base + t, 0, 2 * k + 1])):
                    found[j] = jnp.where(hit, value, found[j])
            start = start + count
        return found

    places = [assigned(0, n) for n in range(NS)]
    source, row0, col0 = places[0]
    for n in range(1, NS):
        source, row0, col0 = (jnp.where(s == n, a, b) for a, b in zip(places[n], (source, row0, col0)))
    _, _, col_prev = assigned(NS, s)

    loads[0].wait()
    for e_ref, re, im, sign in ((e_f, 0, 1, 1), (e_i, 0, 1, -1), (e_h, 2, 3, 1), (e_c, 2, 3, -1)):
        e_ref[0:N, 0:N] = tabs[re]
        e_ref[N:, N:] = tabs[re]
        e_ref[0:N, N:] = -tabs[im] if sign > 0 else tabs[im]
        e_ref[N:, 0:N] = tabs[im] if sign > 0 else -tabs[im]

    def one_hot(shape, rule):
        a, b = lax.broadcasted_iota(jnp.int32, shape, 0), lax.broadcasted_iota(jnp.int32, shape, 1)
        return jnp.where(rule(a, b), 1.0, 0.0).astype(BF)

    def dot(a, b):
        return jnp.dot(a, b, preferred_element_type=F32)

    def col_block(col):
        k = jnp.int32(0)
        for edge in range(1, NS - 1):
            k = k + jnp.where(col >= edge * N, 1, 0)
        return k

    def picks(offset):
        return [one_hot((N, N), lambda a, b: a + h * N == b + offset) for h in range(2)]

    def columns(layer, part, k, pick):
        first, second = tile[layer][k, part].astype(BF), tile[layer][k + 1, part].astype(BF)
        return (dot(first, pick[0]) + dot(second, pick[1])).astype(BF)

    k_prev, k_own = col_block(col_prev), col_block(col0)
    pick_prev = picks(col_prev - k_prev * N)

    pl.semaphore_wait(barrier, len(peers))

    def start(copy):
        copy.start()
        sends.append(copy)

    def meas_copy(q, slot, n, peer):
        ref = meas.at[pl.ds(slot, n)]
        return remote(ref, ref, send.at[q], recv.at[q], (peer, o))

    for q, peer in ((0, partner), (1, right_me), (2, left_me)):
        start(remote(meas_hbm, meas.at[pl.ds(2 * s, 2)], send.at[q], recv.at[q], (peer, o)))

    def halo_copy(layer):
        return remote(hsend.at[layer], hrecv.at[layer], send.at[9 + layer], recv.at[9 + layer], (s, down))

    for layer in range(2):
        for b in range(NS):
            loads[3 + NS * layer + b].wait()
        for part in range(2):
            hsend[layer, part] = columns(layer, part, k_prev, pick_prev)
        start(halo_copy(layer))
    pick_own = picks(col0 - k_own * N)
    for layer in range(2):
        for part in range(2):
            local[layer, part] = columns(layer, part, k_own, pick_own)
    rows_here = one_hot((N, N), lambda a, b: b == a + row0)
    rows_next = one_hot((N, N), lambda a, b: b + N == a + row0)
    turn = jnp.where(col0 == 7 * N, 0, col0 - k_own * N)
    turn_rows = one_hot((N, N), lambda a, b: (b + row0 == a) | (b + row0 == a + N))
    turn_cols = one_hot((N, N), lambda a, b: (a + turn == b) | (a + turn == b + N))
    loads[1].wait()

    def window(layer):
        halo_copy(layer).wait_recv()
        for part in range(2):
            win[layer, part] = dot(rows_here, local[layer, part]) + dot(rows_next, hrecv[layer, part])

    step = 32

    def by_rows(body):
        def run(i, carry):
            body(pl.ds(pl.multiple_of(i * step, step), step), i)
            return carry

        lax.fori_loop(0, N // step, run, 0)

    def put(m, rows, i, re, im):
        v[pl.ds(pl.multiple_of(i * step, step), step), m * N : (m + 1) * N] = re.astype(BF)
        v[pl.ds(pl.multiple_of(N + i * step, step), step), m * N : (m + 1) * N] = im.astype(BF)

    def left_mul(matrix):
        for m in range(2):
            product = dot(matrix[...], v[:, m * N : (m + 1) * N])
            u[m * N : (m + 1) * N, 0:N] = product[0:N].astype(BF)
            u[m * N : (m + 1) * N, N:] = product[N:].astype(BF)

    def right_mul(matrix, result):
        for part in range(2):
            product = dot(u[...], matrix[:, part * N : (part + 1) * N])
            result[0, part] = product[0:N]
            result[1, part] = product[N:]

    window(0)

    def enter(rows, i):
        re, im = win[0, 0, rows, :], win[0, 1, rows, :]
        for m in range(2):
            pr, pi = probe[m, 0, rows, :], probe[m, 1, rows, :]
            put(m, rows, i, pr * re - pi * im, pr * im + pi * re)

    by_rows(enter)
    left_mul(e_h)
    meas_copy(1, 2 * left_me, 2, right_me).wait_recv()
    start(meas_copy(3, 2 * left_me, 1, right_me))
    start(meas_copy(4, 2 * left_me, 2, partner))
    meas_copy(2, 2 * right_me, 2, left_me).wait_recv()
    start(meas_copy(5, 2 * right_me + 1, 1, left_me))
    start(meas_copy(6, 2 * right_me, 2, partner))
    right_mul(e_c, arr)
    window(1)

    def second(rows, i):
        re, im = win[1, 0, rows, :], win[1, 1, rows, :]
        for m in range(2):
            pr, pi = arr[m, 0, rows, :], arr[m, 1, rows, :]
            put(m, rows, i, pr * re - pi * im, pr * im + pi * re)

    by_rows(second)
    meas_copy(3, 2 * far_me, 1, right_me).wait_recv()
    start(meas_copy(7, 2 * far_me, 1, partner))
    meas_copy(5, 2 * far_me + 1, 1, left_me).wait_recv()
    start(meas_copy(8, 2 * far_me + 1, 1, partner))
    left_mul(e_f)
    right_mul(e_i, far)
    loads[2].wait()
    meas_copy(0, 2 * partner, 2, partner).wait_recv()
    meas_copy(4, 2 * left_ot, 2, partner).wait_recv()
    meas_copy(6, 2 * right_ot, 2, partner).wait_recv()
    meas_copy(7, 2 * far_ot, 1, partner).wait_recv()
    meas_copy(8, 2 * far_ot + 1, 1, partner).wait_recv()

    pattern[...] = meas[source]

    def misfit(rows, i):
        parts = [(far[m, 0, rows, :], far[m, 1, rows, :]) for m in range(2)]
        total = parts[0][0] ** 2 + parts[0][1] ** 2 + (parts[1][0] ** 2 + parts[1][1] ** 2)
        gap = total - pattern[rows, :].astype(F32)
        for m in range(2):
            put(m, rows, i, gap * parts[m][0], gap * parts[m][1])

    by_rows(misfit)
    left_mul(e_i)
    right_mul(e_f, cur)

    def near(layer, c, side):
        q = 11 + 18 * layer + (2 if side else 4)
        peer = (right if side else left)[c]
        return remote(
            gsend.at[layer, c], wins.at[layer, s], send.at[q + c], recv.at[q + core], (peer, o)
        )

    def near_in(layer, c, side):
        q = 11 + 18 * layer + (2 if side else 4)
        slot = wins.at[layer, (left if side else right)[c]]
        return remote(slot, slot, send.at[q + c], recv.at[q + c], (partner, o))

    def relay(layer, c, side, incoming=False):
        q = 11 + 18 * layer + (6 if side else 8) + c
        owner = far_at[c] if incoming else (left if side else right)[c]
        half = wins.at[layer, owner, pl.ds(0 if side else N // 2, N // 2)]
        return remote(half, half, send.at[q], recv.at[q], (right_me if side else left_me, o))

    def pair(layer, incoming=False):
        q = 11 + 18 * layer
        slot = wins.at[layer, partner if incoming else s]
        return remote(gsend.at[layer, other], slot, send.at[q], recv.at[q], (partner, o))

    def share(layer, first, adjoint):
        for part in range(2):
            if part == 0:
                term = lambda m: first[m, 0] * adjoint[m, 0] + first[m, 1] * adjoint[m, 1]
            else:
                term = lambda m: first[m, 0] * adjoint[m, 1] - first[m, 1] * adjoint[m, 0]
            grad = (term(0) + term(1)).astype(BF)
            gsend[layer, part] = dot(dot(turn_rows, grad).astype(BF), turn_cols).astype(BF)
        start(pair(layer))
        for c in range(2):
            start(near(layer, c, 1))
            start(near(layer, c, 0))
        wins[layer, s] = gsend[layer, core]

    def pass_on(layer):
        for side in (1, 0):
            for c in range(2):
                near_in(layer, c, side).wait_recv()
                start(relay(layer, c, side))

    share(1, arr, cur)

    def behind(rows, i):
        re, im = win[1, 0, rows, :], win[1, 1, rows, :]
        for m in range(2):
            cr, ci = cur[m, 0, rows, :], cur[m, 1, rows, :]
            put(m, rows, i, re * cr + im * ci, re * ci - im * cr)

    by_rows(behind)
    left_mul(e_c)
    right_mul(e_h, cur)
    share(0, probe, cur)

    def leave(rows, i):
        re, im = win[0, 0, rows, :], win[0, 1, rows, :]
        for m in range(2):
            cr, ci = cur[m, 0, rows, :], cur[m, 1, rows, :]
            esend[m, 0, rows, :] = (re * cr + im * ci).astype(BF)
            esend[m, 1, rows, :] = (re * ci - im * cr).astype(BF)

    by_rows(leave)
    q_pair, q_y, q_z, q_x = 53, 54, 57, 64
    e_copy = remote(esend.at[other], erecv, send.at[q_pair], recv.at[q_pair], (partner, o))
    start(e_copy)
    pass_on(1)
    e_copy.wait_recv()

    def add_pair(rows, i):
        for part in range(2):
            ysend[part, rows, :] = (esend[core, part, rows, :].astype(F32) + erecv[part, rows, :].astype(F32)).astype(BF)

    by_rows(add_pair)
    deep = N // NY
    y_copies = []
    for k in range(1, NY):
        y_to = rem(y + k, NY)
        rows_to = pl.ds(pl.multiple_of(y_to * deep, deep), deep)
        copy = remote(
            ysend.at[:, rows_to, :], yrecv.at[k - 1], send.at[q_y + k - 1], recv.at[q_y + k - 1], (s, y_to * NZ + z)
        )
        start(copy)
        y_copies.append(copy)

    lane = lax.broadcasted_iota(jnp.int32, (1, N), 1)

    def gather(layer):
        chunk = 16
        cols = [[(lane + (2 * x + b) * N >= c0) & (lane + (2 * x + b) * N < c0 + N) for b in range(2)] for _, _, c0 in places]
        cols = [[jnp.where(mask, 1.0, 0.0).astype(F32) for mask in pair_masks] for pair_masks in cols]

        def run(i, carry):
            rows = pl.ds(pl.multiple_of(i * chunk, chunk), chunk)
            line = lax.broadcasted_iota(jnp.int32, (chunk, N), 0) + i * chunk
            sums = [[jnp.zeros((chunk, N), F32) for _ in range(2)] for _ in range(2)]
            for n in range(NS):
                term = wins[layer, n, rows, :].astype(F32)
                above = line >= places[n][1]
                for b in range(2):
                    masked = term * cols[n][b]
                    sums[b][0] = sums[b][0] + jnp.where(above, masked, 0.0)
                    sums[b][1] = sums[b][1] + jnp.where(above, 0.0, masked)
            mine = core == 0
            acc[layer, rows, :] = jnp.where(mine, sums[0][0], sums[1][0])
            tsend[layer, rows, :] = jnp.where(mine, sums[1][0], sums[0][0]).astype(BF)
            for b in range(2):
                bsend[layer, b, rows, :] = sums[b][1].astype(BF)
            return carry

        lax.fori_loop(0, N // chunk, run, 0)

    def top_copy(layer):
        q = 71 + layer
        return remote(tsend.at[layer], trecv.at[layer], send.at[q], recv.at[q], (partner, o))

    def bottom_copy(layer, b):
        q = 73 + 2 * layer
        return remote(bsend.at[layer, b], brecv.at[layer, core], send.at[q + b], recv.at[q + core], (2 * x + b, up))

    def bottom_in(layer, c):
        q = 73 + 2 * layer
        return remote(bsend.at[layer, c], brecv.at[layer, c], send.at[q + c], recv.at[q + c], (s, up))

    def collect(layer):
        pair(layer, True).wait_recv()
        for side in (1, 0):
            for c in range(2):
                relay(layer, c, side, True).wait_recv()
        gather(layer)
        for b in range(2):
            start(bottom_copy(layer, b))
        start(top_copy(layer))

    def finish(layer):
        top_copy(layer).wait_recv()
        for c in range(2):
            bottom_in(layer, c).wait_recv()
        for i in range(N // 64):
            rows = pl.ds(i * 64, 64)
            out_ref[layer, core, rows, :] = acc[layer, rows, :] + brecv[layer, core, rows, :].astype(F32)
            out_ref[layer, other, rows, :] = (
                trecv[layer, rows, :].astype(F32) + brecv[layer, other, rows, :].astype(F32)
            )

    collect(1)
    for copy in y_copies:
        copy.wait_recv()
    rows_me = pl.ds(pl.multiple_of(y * deep, deep), deep)
    for part in range(2):
        total = ysend[part, rows_me, :].astype(F32)
        for k in range(NY - 1):
            total = total + yrecv[k, part].astype(F32)
        zsend[part] = total
    z_copies = []
    for k in range(1, NZ):
        z_to = rem(z + k, NZ)
        copy = remote(
            zsend.at[:, pl.ds(pl.multiple_of(z_to * 8, 8), 8), :], zrecv.at[k - 1],
            send.at[q_z + k - 1], recv.at[q_z + k - 1], (s, y * NZ + z_to),
        )
        start(copy)
        z_copies.append(copy)
    pass_on(0)
    for copy in z_copies:
        copy.wait_recv()
    for part in range(2):
        total = zsend[part, pl.ds(pl.multiple_of(z * 8, 8), 8), :]
        for k in range(NZ - 1):
            total = total + zrecv[k, part]
        xsend[part] = total
    x_copies = []
    for k in range(1, NS):
        copy = remote(xsend, xrecv.at[k - 1], send.at[q_x + k - 1], recv.at[q_x + k - 1], (rem(s + k, NS), o))
        start(copy)
        x_copies.append(copy)
    collect(0)
    for copy in x_copies:
        copy.wait_recv()
    factor = 1.0 / math.sqrt(256.0)
    mine, theirs = xsend[...], xrecv[0]
    for k in range(2, NS):
        if k % 2:
            theirs = theirs + xrecv[k - 1]
        else:
            mine = mine + xrecv[k - 1]
    pout_ref[core] = mine * factor
    pout_ref[other] = theirs * factor
    finish(1)
    finish(0)
    for copy in sends:
        copy.wait_send()


def body(object_slices, probe, measured, positions, counts):
    table = pl.pallas_call(
        table_kernel,
        out_shape=jax.ShapeDtypeStruct((2 * NS, 1, 128), jnp.int32),
        in_specs=[pl.BlockSpec(memory_space=pltpu.SMEM)] * 2,
        out_specs=pl.BlockSpec(memory_space=pltpu.VMEM),
        scratch_shapes=[
            pltpu.VMEM((1, 128), jnp.int32),
            pltpu.VMEM((2 * NS, 1, 128), jnp.int32),
            pltpu.SemaphoreType.DMA((2 * NS,)),
            pltpu.SemaphoreType.DMA((2 * NS,)),
        ],
        compiler_params=pltpu.CompilerParams(collective_id=0, has_side_effects=True),
        name="places",
    )(positions[0, 0], counts)

    vmem = pltpu.VMEM
    square = lambda *lead: (*lead, N, N)
    any_spec = pl.BlockSpec(memory_space=pl.ANY)
    object_grad, probe_rows = pl.pallas_call(
        main_kernel,
        out_shape=(
            jax.ShapeDtypeStruct(square(2, 2), F32),
            jax.ShapeDtypeStruct((2, 2, 8, N), F32),
        ),
        in_specs=[pl.BlockSpec(memory_space=pltpu.SMEM), any_spec, any_spec, any_spec, any_spec],
        out_specs=(pl.BlockSpec(memory_space=vmem), pl.BlockSpec(memory_space=vmem)),
        scratch_shapes=[
            *[vmem(square(NS, 2), F32)] * 2,
            vmem(square(2, 2), F32),
            vmem(square(16), BF),
            vmem(square(4), BF),
            *[vmem((2 * N, 2 * N), BF)] * 4,
            vmem(square(2, 2), BF),
            vmem(square(2, 2), BF),
            vmem(square(2, 2), BF),
            vmem(square(), BF),
            vmem(square(2, 2), F32),
            vmem((2 * N, 2 * N), BF),
            vmem((2 * N, 2 * N), BF),
            vmem(square(2, 2), F32),
            vmem(square(2, 2), F32),
            vmem(square(2, 2), F32),
            vmem(square(2, 2), BF),
            vmem(square(2, NS), BF),
            vmem(square(2), F32),
            vmem(square(2), BF),
            vmem(square(2), BF),
            vmem(square(2, 2), BF),
            vmem(square(2, 2), BF),
            vmem(square(2, 2), BF),
            vmem(square(2), BF),
            vmem(square(2), BF),
            vmem((NY - 1, 2, N // NY, N), BF),
            vmem((2, N // NY, N), F32),
            vmem((NZ - 1, 2, 8, N), F32),
            vmem((2, 8, N), F32),
            vmem((NS - 1, 2, 8, N), F32),
            pltpu.SemaphoreType.DMA((3 + 2 * NS,)),
            pltpu.SemaphoreType.DMA((77,)),
            pltpu.SemaphoreType.DMA((77,)),
        ],
        compiler_params=pltpu.CompilerParams(
            collective_id=1, has_side_effects=True, vmem_limit_bytes=60 * 1024 * 1024
        ),
        name="gradient",
    )(table, object_slices, probe, measured[0, 0], tables())
    cols = lax.axis_index("scan") * 32
    return object_grad, lax.dynamic_slice_in_dim(probe_rows, cols, 32, axis=3)


def solution(mesh):
    return jax.shard_map(
        body,
        mesh=mesh,
        in_specs=(
            P(None, None, "obj", None),
            P(),
            P("scan", "obj", None, None, None),
            P("scan", "obj", None, None),
            P("scan", "obj"),
        ),
        out_specs=(P(None, None, "obj", "scan"), P(None, None, "obj", "scan")),
        check_vma=False,
    )
```

time: 733 us -> 81.3 us (0.11)
  waiting for transfers between devices: 535 us -> 0 us
  Pallas kernels: 0 us -> 76.1 us
  local copies, waits for them, and re-layouts: 79.2 us -> 3.69 us
  other arithmetic: 55.3 us -> 0 us
  matrix products: 29.5 us -> 0 us
  between operations: 14.5 us -> 1.3 us
  starting transfers between devices: 9.05 us -> 0 us
  loops' own time: 8.3 us -> 0 us
    reduce_scatter x2 -> x0, waiting for transfers between devices: 341 us -> none  [the longest x1 284 us: body(): lax.psum_scatter(probe_sum, 'obj', scatter_dimension=2, tiled=True)]
    ppermute x2 -> x0, waiting for transfers between devices: 171 us -> none  [shifted(): return lax.ppermute(block, axis, route)]
    pallas_call x0 -> x2, Pallas kernels: none -> 76.1 us  [the longest x1 59.9 us: body(): pl.pallas_call(main_kernel, out_shape=(jax.ShapeDtypeStruct(square(2, 2),...]
    dot_general x12 -> x0, matrix products: 29.5 us -> none  [transform(): jnp.einsum('qab,pqbc->pac', partial_out.astype(jnp.bfloat16), matrix, pre...]
    dynamic_update_slice x4 -> x0, local copies, waits for them, and re-layouts: 24.4 us -> none  [the longest x2 24.2 us: add_window(): return (lax.dynamic_update_slice(band, current + patch_grad, corner), None)]
    unnamed x4 -> x0, waiting for transfers between devices: 23.3 us -> none
    add x9 -> x0, other arithmetic: 21.8 us -> none  [the longest x1 11.7 us: body(): tile_grad = band[:, :, :tile_rows].at[:, :, :length].add(rim_back)]
    another operation x17 -> x0, other arithmetic: 15.4 us -> none
  transfers between devices with their start and end apart: 5 -> 0, of which waited for: 4 -> 0; matrix products, arithmetic and copies ran while one was open for 3% -> 0% of each run, Pallas kernels for 0% -> 0%
where the time goes in v1:
time: 81.3 us; the launch traced here: 81.1 us
  Pallas kernels  76.1 us (94%)
  local copies, waits for them, and re-layouts  3.69 us (5%)
  between operations  1.3 us (2%)
    pallas_call x1, Pallas kernels, body(): pl.pallas_call(main_kernel, out_shape=(jax.ShapeDtypeStruct(square(2, 2),...  59.9 us
    pallas_call x1, Pallas kernels, body(): pl.pallas_call(table_kernel, out_shape=jax.ShapeDtypeStruct((2 * NS, 1, 1...  16.2 us
    unnamed x1, local copies, waits for them, and re-layouts  2.28 us

profile of v1, /device:TPU:1, one launch (start us, length us, event | category | flops | bytes accessed | tf_op | source)
XLA Modules:
  0.0 81.1 jit_solution(13687755566174093667)
XLA Ops:
  1.3 16.2 %places.1.tab = s32[16,1,128]{2,1,0:T(1,128)} custom-call(s32[2,2]{1,0:T(2,128)} %bitcast.3, s32[1,1]{1,0:T(1,128)S(6)} %copy.9.count_ref), custom_call_target="tpu_custom_call" | custom-call | tf_op jit(solution)/shard_map/places/pallas_call | solution.py:473
  17.5 59.9 %gradient.1 = (f32[2,2,256,256]{3,2,1,0:T(8,128)}, f32[2,2,8,256]{3,2,1,0:T(8,128)}) custom-call(s32[16,1,128]{2,1,0:T(1,128)} %places.1.tab, f32[2,2,256,2048]{3,2,1,0:T(8,128)} %tile_hbm.1, f32[2,2,256,256]{3,2,1,0:T(8,128)} %probe_hbm.1, bf16[2,256,256]{2,1,0:T(8,128)(2,1)} %bitcast.2, bf16[4,256,256]{2,1,0:T(8,128)(2,1)} %constant.14.clone.table_hbm), custom_call_target="tpu_custom_call" | custom-call | tf_op jit(solution)/shard_map/gradient/pallas_call | solution.py:491
  77.4 1.4 %constant_dynamic-slice_fusion = f32[2,2,8,32]{3,2,1,0:T(8,128)} fusion(f32[2,2,8,256]{3,2,1,0:T(8,128)} %get-tuple-element.5, s32[]{:T(128)S(6)} %select_n.3), kind=kLoop, calls=%fused_computation | loop fusion | bytes 8196 | tf_op jit(solution)/shard_map/dynamic_slice | solution.py:540
  78.8 2.3 %copy.10 = f32[2,2,256,256]{3,2,1,0:T(8,128)} copy(f32[2,2,256,256]{3,2,1,0:T(8,128)} %get-tuple-element.8) | data formatting | bytes 2097152

commit v2 on v1

--- a/solution.py
+++ b/solution.py
@@ -38,41 +38,9 @@
     )
 
 
-def table_kernel(pos_ref, count_ref, out_ref, row_ref, tab_ref, send, recv):
-    s, o = lax.axis_index("scan"), lax.axis_index("obj")
-    up, down = rem(o + 1, NO), rem(o + NO - 1, NO)
-    barrier = pltpu.get_barrier_semaphore()
-    for k in range(NS):
-        if k:
-            pl.semaphore_signal(barrier, inc=1, device_id=(rem(s + k, NS), o), device_id_type=MESH)
-        pl.semaphore_signal(barrier, inc=1, device_id=(rem(s + k, NS), down), device_id_type=MESH)
-    lane = lax.broadcasted_iota(jnp.int32, (1, 128), 1)
-    row = jnp.zeros((1, 128), jnp.int32)
-    for j, value in enumerate((pos_ref[0, 0], pos_ref[0, 1], pos_ref[1, 0], pos_ref[1, 1], count_ref[0, 0])):
-        row = jnp.where(lane == j, value, row)
-    row_ref[...] = row
-    tab_ref[s] = row
-    pl.semaphore_wait(barrier, 2 * NS - 1)
-    copies = []
-    for k in range(NS):
-        peer = rem(s + k, NS)
-        source = rem(s + NS - k, NS)
-        if k:
-            copy = remote(row_ref, tab_ref.at[s], send.at[k], recv.at[k], (peer, o))
-            copy.start()
-            copies.append((copy, remote(row_ref, tab_ref.at[source], send.at[k], recv.at[k], (peer, o))))
-        copy = remote(row_ref, tab_ref.at[NS + s], send.at[NS + k], recv.at[NS + k], (peer, up))
-        copy.start()
-        copies.append((copy, remote(row_ref, tab_ref.at[NS + source], send.at[NS + k], recv.at[NS + k], (peer, up))))
-    for sent, landed in copies:
-        sent.wait_send()
-        landed.wait_recv()
-    out_ref[...] = tab_ref[...]
-
-
 def main_kernel(
-    tab, tile_hbm, probe_hbm, meas_hbm, table_hbm, out_ref, pout_ref,
-    tile_0, tile_1, probe, meas, tabs, e_f, e_i, e_h, e_c, hsend, hrecv, local, pattern, win, v, u, arr, far, cur,
+    pos_ref, count_ref, tile_hbm, probe_hbm, meas_hbm, table_hbm, out_ref, pout_ref,
+    row, rows_in, tab, tile_0, tile_1, probe, meas, tabs, e_f, e_i, e_h, e_c, hsend, hrecv, local, pattern, win, v, u, arr, far, cur,
     gsend, wins, acc, tsend, trecv, bsend, brecv, esend, erecv, ysend, yrecv, zsend, zrecv, xsend, xrecv,
     dma, send, recv,
 ):
@@ -106,11 +74,72 @@
 
     barrier = pltpu.get_barrier_semaphore()
     peers = [(rem(s + k, NS), o) for k in range(1, NS)]
-    peers += [(s, up), (s, down), (partner, down)]
+    peers += [(s, up)] + [(rem(s + k, NS), down) for k in range(NS)]
     peers += [(s, rem(y + k, NY) * NZ + z) for k in range(1, NY)]
     peers += [(s, y * NZ + rem(z + k, NZ)) for k in range(1, NZ)]
     for peer in peers:
         pl.semaphore_signal(barrier, inc=1, device_id=peer, device_id_type=MESH)
+
+    lane = lax.broadcasted_iota(jnp.int32, (1, 128), 1)
+    line = jnp.zeros((1, 128), jnp.int32)
+    for j, value in enumerate((pos_ref[0, 0], pos_ref[0, 1], pos_ref[1, 0], pos_ref[1, 1], count_ref[0, 0])):
+        line = jnp.where(lane == j, value, line)
+    row[...] = line
+    rows_in[s] = line
+
+    loads[0].wait()
+    for e_ref, re, im, sign in ((e_f, 0, 1, 1), (e_i, 0, 1, -1), (e_h, 2, 3, 1), (e_c, 2, 3, -1)):
+        e_ref[0:N, 0:N] = tabs[re]
+        e_ref[N:, N:] = tabs[re]
+        e_ref[0:N, N:] = -tabs[im] if sign > 0 else tabs[im]
+        e_ref[N:, 0:N] = tabs[im] if sign > 0 else -tabs[im]
+
+    def one_hot(shape, rule):
+        a, b = lax.broadcasted_iota(jnp.int32, shape, 0), lax.broadcasted_iota(jnp.int32, shape, 1)
+        return jnp.where(rule(a, b), 1.0, 0.0).astype(BF)
+
+    def dot(a, b):
+        return jnp.dot(a, b, preferred_element_type=F32)
+
+    def col_block(col):
+        k = jnp.int32(0)
+        for edge in range(1, NS - 1):
+            k = k + jnp.where(col >= edge * N, 1, 0)
+        return k
+
+    def picks(offset):
+        return [one_hot((N, N), lambda a, b: a + h * N == b + offset) for h in range(2)]
+
+    def columns(layer, part, k, pick):
+        first, second = tile[layer][k, part].astype(BF), tile[layer][k + 1, part].astype(BF)
+        return (dot(first, pick[0]) + dot(second, pick[1])).astype(BF)
+
+
+    pl.semaphore_wait(barrier, len(peers))
+
+    def start(copy):
+        copy.start()
+        sends.append(copy)
+
+    def meas_copy(q, slot, n, peer):
+        ref = meas.at[pl.ds(slot, n)]
+        return remote(ref, ref, send.at[q], recv.at[q], (peer, o))
+
+    def place_copy(k, base, owner):
+        peer = (rem(s + k, NS), up if base else o)
+        return remote(row, rows_in.at[base + owner], send.at[77 + base + k], recv.at[77 + base + k], peer)
+
+    every = [(k, base) for base in (0, NS) for k in range(NS) if base or k]
+    for k, base in every:
+        start(place_copy(k, base, s))
+    for q, peer in ((0, partner), (1, right_me), (2, left_me)):
+        start(remote(meas_hbm, meas.at[pl.ds(2 * s, 2)], send.at[q], recv.at[q], (peer, o)))
+
+    for k, base in every:
+        place_copy(k, base, rem(s + NS - k, NS)).wait_recv()
+    fetch = pltpu.make_async_copy(rows_in, tab, dma.at[3 + 2 * NS])
+    fetch.start()
+    fetch.wait()
 
     def assigned(base, n):
         start, found = jnp.int32(0), [jnp.int32(0)] * 3
@@ -129,48 +158,8 @@
         source, row0, col0 = (jnp.where(s == n, a, b) for a, b in zip(places[n], (source, row0, col0)))
     _, _, col_prev = assigned(NS, s)
 
-    loads[0].wait()
-    for e_ref, re, im, sign in ((e_f, 0, 1, 1), (e_i, 0, 1, -1), (e_h, 2, 3, 1), (e_c, 2, 3, -1)):
-        e_ref[0:N, 0:N] = tabs[re]
-        e_ref[N:, N:] = tabs[re]
-        e_ref[0:N, N:] = -tabs[im] if sign > 0 else tabs[im]
-        e_ref[N:, 0:N] = tabs[im] if sign > 0 else -tabs[im]
-
-    def one_hot(shape, rule):
-        a, b = lax.broadcasted_iota(jnp.int32, shape, 0), lax.broadcasted_iota(jnp.int32, shape, 1)
-        return jnp.where(rule(a, b), 1.0, 0.0).astype(BF)
-
-    def dot(a, b):
-        return jnp.dot(a, b, preferred_element_type=F32)
-
-    def col_block(col):
-        k = jnp.int32(0)
-        for edge in range(1, NS - 1):
-            k = k + jnp.where(col >= edge * N, 1, 0)
-        return k
-
-    def picks(offset):
-        return [one_hot((N, N), lambda a, b: a + h * N == b + offset) for h in range(2)]
-
-    def columns(layer, part, k, pick):
-        first, second = tile[layer][k, part].astype(BF), tile[layer][k + 1, part].astype(BF)
-        return (dot(first, pick[0]) + dot(second, pick[1])).astype(BF)
-
     k_prev, k_own = col_block(col_prev), col_block(col0)
     pick_prev = picks(col_prev - k_prev * N)
-
-    pl.semaphore_wait(barrier, len(peers))
-
-    def start(copy):
-        copy.start()
-        sends.append(copy)
-
-    def meas_copy(q, slot, n, peer):
-        ref = meas.at[pl.ds(slot, n)]
-        return remote(ref, ref, send.at[q], recv.at[q], (peer, o))
-
-    for q, peer in ((0, partner), (1, right_me), (2, left_me)):
-        start(remote(meas_hbm, meas.at[pl.ds(2 * s, 2)], send.at[q], recv.at[q], (peer, o)))
 
     def halo_copy(layer):
         return remote(hsend.at[layer], hrecv.at[layer], send.at[9 + layer], recv.at[9 + layer], (s, down))
@@ -470,21 +459,6 @@
 
 
 def body(object_slices, probe, measured, positions, counts):
-    table = pl.pallas_call(
-        table_kernel,
-        out_shape=jax.ShapeDtypeStruct((2 * NS, 1, 128), jnp.int32),
-        in_specs=[pl.BlockSpec(memory_space=pltpu.SMEM)] * 2,
-        out_specs=pl.BlockSpec(memory_space=pltpu.VMEM),
-        scratch_shapes=[
-            pltpu.VMEM((1, 128), jnp.int32),
-            pltpu.VMEM((2 * NS, 1, 128), jnp.int32),
-            pltpu.SemaphoreType.DMA((2 * NS,)),
-            pltpu.SemaphoreType.DMA((2 * NS,)),
-        ],
-        compiler_params=pltpu.CompilerParams(collective_id=0, has_side_effects=True),
-        name="places",
-    )(positions[0, 0], counts)
-
     vmem = pltpu.VMEM
     square = lambda *lead: (*lead, N, N)
     any_spec = pl.BlockSpec(memory_space=pl.ANY)
@@ -494,9 +468,12 @@
             jax.ShapeDtypeStruct(square(2, 2), F32),
             jax.ShapeDtypeStruct((2, 2, 8, N), F32),
         ),
-        in_specs=[pl.BlockSpec(memory_space=pltpu.SMEM), any_spec, any_spec, any_spec, any_spec],
+        in_specs=[pl.BlockSpec(memory_space=pltpu.SMEM)] * 2 + [any_spec] * 4,
         out_specs=(pl.BlockSpec(memory_space=vmem), pl.BlockSpec(memory_space=vmem)),
         scratch_shapes=[
+            vmem((1, 128), jnp.int32),
+            vmem((2 * NS, 1, 128), jnp.int32),
+            pltpu.SMEM((2 * NS, 1, 128), jnp.int32),
             *[vmem(square(NS, 2), F32)] * 2,
             vmem(square(2, 2), F32),
             vmem(square(16), BF),
@@ -527,15 +504,15 @@
             vmem((NZ - 1, 2, 8, N), F32),
             vmem((2, 8, N), F32),
             vmem((NS - 1, 2, 8, N), F32),
-            pltpu.SemaphoreType.DMA((3 + 2 * NS,)),
-            pltpu.SemaphoreType.DMA((77,)),
-            pltpu.SemaphoreType.DMA((77,)),
+            pltpu.SemaphoreType.DMA((4 + 2 * NS,)),
+            pltpu.SemaphoreType.DMA((93,)),
+            pltpu.SemaphoreType.DMA((93,)),
         ],
         compiler_params=pltpu.CompilerParams(
-            collective_id=1, has_side_effects=True, vmem_limit_bytes=60 * 1024 * 1024
+            collective_id=0, has_side_effects=True, vmem_limit_bytes=60 * 1024 * 1024
         ),
         name="gradient",
-    )(table, object_slices, probe, measured[0, 0], tables())
+    )(positions[0, 0], counts, object_slices, probe, measured[0, 0], tables())
     cols = lax.axis_index("scan") * 32
     return object_grad, lax.dynamic_slice_in_dim(probe_rows, cols, 32, axis=3)
 

time: 81.3 us -> 78.9 us (0.970)
  Pallas kernels: 76.1 us -> 73.7 us
    pallas_call x1 -> x0, Pallas kernels: 16.2 us -> none  [body(): pl.pallas_call(table_kernel, out_shape=jax.ShapeDtypeStruct((2 * NS, 1, 1...]
    pallas_call x1, Pallas kernels: 59.9 us -> 73.7 us  [body(): pl.pallas_call(main_kernel, out_shape=(jax.ShapeDtypeStruct(square(2, 2),...]
where the time goes in v2:
time: 78.9 us; the launch traced here: 78.7 us
  Pallas kernels  73.7 us (93%)
  local copies, waits for them, and re-layouts  3.69 us (5%)
  between operations  1.29 us (2%)
    pallas_call x1, Pallas kernels, body(): pl.pallas_call(main_kernel, out_shape=(jax.ShapeDtypeStruct(square(2, 2),...  73.7 us
    unnamed x1, local copies, waits for them, and re-layouts  2.28 us

profile of v2, /device:TPU:1, one launch (start us, length us, event | category | flops | bytes accessed | tf_op | source)
XLA Modules:
  0.0 78.7 jit_solution(12309658722707968521)
XLA Ops:
  1.3 73.7 %gradient.1 = (f32[2,2,256,256]{3,2,1,0:T(8,128)}, f32[2,2,8,256]{3,2,1,0:T(8,128)}) custom-call(s32[2,2]{1,0:T(2,128)} %bitcast.3, s32[1,1]{1,0:T(1,128)S(6)} %copy.9.count_ref, f32[2,2,256,2048]{3,2,1,0:T(8,128)} %tile_hbm.1, f32[2,2,256,256]{3,2,1,0:T(8,128)} %probe_hbm.1, bf16[2,256,256]{2,1,0:T(8,128)(2,1)} %bitcast.2, ...), custom_call_target="tpu_custom_call" | custom-call | tf_op jit(solution)/shard_map/gradient/pallas_call | solution.py:465
  75.0 1.4 %constant_dynamic-slice_fusion = f32[2,2,8,32]{3,2,1,0:T(8,128)} fusion(f32[2,2,8,256]{3,2,1,0:T(8,128)} %get-tuple-element.5, s32[]{:T(128)S(6)} %select_n.3), kind=kLoop, calls=%fused_computation | loop fusion | bytes 8196 | tf_op jit(solution)/shard_map/dynamic_slice | solution.py:517
  76.4 2.3 %copy.10 = f32[2,2,256,256]{3,2,1,0:T(8,128)} copy(f32[2,2,256,256]{3,2,1,0:T(8,128)} %get-tuple-element.8) | data formatting | bytes 2097152

commit v3 on v2

--- a/solution.py
+++ b/solution.py
@@ -41,7 +41,7 @@
 def main_kernel(
     pos_ref, count_ref, tile_hbm, probe_hbm, meas_hbm, table_hbm, out_ref, pout_ref,
     row, rows_in, tab, tile_0, tile_1, probe, meas, tabs, e_f, e_i, e_h, e_c, hsend, hrecv, local, pattern, win, v, u, arr, far, cur,
-    gsend, wins, acc, tsend, trecv, bsend, brecv, esend, erecv, ysend, yrecv, zsend, zrecv, xsend, xrecv,
+    gsend, wins, acc, tsend, trecv, bsend, brecv, esend, erecv, ysend, yrecv, zsend, zrecv, xall,
     dma, send, recv,
 ):
     s, o = lax.axis_index("scan"), lax.axis_index("obj")
@@ -60,6 +60,14 @@
     tile = (tile_0, tile_1)
     sends = []
 
+    barrier = pltpu.get_barrier_semaphore()
+    peers = [(rem(s + k, NS), o) for k in range(1, NS)]
+    peers += [(s, up)] + [(rem(s + k, NS), down) for k in range(NS)]
+    peers += [(s, rem(y + k, NY) * NZ + z) for k in range(1, NY)]
+    peers += [(s, y * NZ + rem(z + k, NZ)) for k in range(1, NZ)]
+    for peer in peers:
+        pl.semaphore_signal(barrier, inc=1, device_id=peer, device_id_type=MESH)
+
     loads = [
         pltpu.make_async_copy(table_hbm, tabs, dma.at[0]),
         pltpu.make_async_copy(probe_hbm, probe, dma.at[1]),
@@ -72,14 +80,6 @@
     for load in loads:
         load.start()
 
-    barrier = pltpu.get_barrier_semaphore()
-    peers = [(rem(s + k, NS), o) for k in range(1, NS)]
-    peers += [(s, up)] + [(rem(s + k, NS), down) for k in range(NS)]
-    peers += [(s, rem(y + k, NY) * NZ + z) for k in range(1, NY)]
-    peers += [(s, y * NZ + rem(z + k, NZ)) for k in range(1, NZ)]
-    for peer in peers:
-        pl.semaphore_signal(barrier, inc=1, device_id=peer, device_id_type=MESH)
-
     lane = lax.broadcasted_iota(jnp.int32, (1, 128), 1)
     line = jnp.zeros((1, 128), jnp.int32)
     for j, value in enumerate((pos_ref[0, 0], pos_ref[0, 1], pos_ref[1, 0], pos_ref[1, 1], count_ref[0, 0])):
@@ -127,18 +127,17 @@
 
     def place_copy(k, base, owner):
         peer = (rem(s + k, NS), up if base else o)
-        return remote(row, rows_in.at[base + owner], send.at[77 + base + k], recv.at[77 + base + k], peer)
+        return remote(row, rows_in.at[base + owner], send.at[85 + base + k], recv.at[85 + base + k], peer)
 
     every = [(k, base) for base in (0, NS) for k in range(NS) if base or k]
     for k, base in every:
         start(place_copy(k, base, s))
-    for q, peer in ((0, partner), (1, right_me), (2, left_me)):
-        start(remote(meas_hbm, meas.at[pl.ds(2 * s, 2)], send.at[q], recv.at[q], (peer, o)))
-
     for k, base in every:
         place_copy(k, base, rem(s + NS - k, NS)).wait_recv()
     fetch = pltpu.make_async_copy(rows_in, tab, dma.at[3 + 2 * NS])
     fetch.start()
+    for q, peer in ((0, partner), (1, right_me), (2, left_me)):
+        start(remote(meas_hbm, meas.at[pl.ds(2 * s, 2)], send.at[q], recv.at[q], (peer, o)))
     fetch.wait()
 
     def assigned(base, n):
@@ -263,28 +262,35 @@
     left_mul(e_i)
     right_mul(e_f, cur)
 
-    def near(layer, c, side):
-        q = 11 + 18 * layer + (2 if side else 4)
+    half = N // 2
+    chunks = [(1, 0), (1, 1), (0, 0), (0, 1)]
+
+    def span(j, part=None):
+        first = chunks[j][1] * half
+        return pl.ds(first, half) if part is None else pl.ds(first + part * half // 2, half // 2)
+
+    def near(j, c, side):
+        layer, q = chunks[j][0], 11 + 14 * j + (2 if side else 4)
         peer = (right if side else left)[c]
         return remote(
-            gsend.at[layer, c], wins.at[layer, s], send.at[q + c], recv.at[q + core], (peer, o)
+            gsend.at[layer, c, span(j)], wins.at[layer, s, span(j)], send.at[q + c], recv.at[q + core], (peer, o)
         )
 
-    def near_in(layer, c, side):
-        q = 11 + 18 * layer + (2 if side else 4)
-        slot = wins.at[layer, (left if side else right)[c]]
+    def near_in(j, c, side):
+        layer, q = chunks[j][0], 11 + 14 * j + (2 if side else 4)
+        slot = wins.at[layer, (left if side else right)[c], span(j)]
         return remote(slot, slot, send.at[q + c], recv.at[q + c], (partner, o))
 
-    def relay(layer, c, side, incoming=False):
-        q = 11 + 18 * layer + (6 if side else 8) + c
+    def relay(j, c, side, incoming=False):
+        q = 11 + 14 * j + (6 if side else 8) + c
         owner = far_at[c] if incoming else (left if side else right)[c]
-        half = wins.at[layer, owner, pl.ds(0 if side else N // 2, N // 2)]
-        return remote(half, half, send.at[q], recv.at[q], (right_me if side else left_me, o))
-
-    def pair(layer, incoming=False):
-        q = 11 + 18 * layer
-        slot = wins.at[layer, partner if incoming else s]
-        return remote(gsend.at[layer, other], slot, send.at[q], recv.at[q], (partner, o))
+        piece = wins.at[chunks[j][0], owner, span(j, 0 if side else 1)]
+        return remote(piece, piece, send.at[q], recv.at[q], (right_me if side else left_me, o))
+
+    def pair(j, incoming=False):
+        layer, q = chunks[j][0], 11 + 14 * j
+        slot = wins.at[layer, partner if incoming else s, span(j)]
+        return remote(gsend.at[layer, other, span(j)], slot, send.at[q], recv.at[q], (partner, o))
 
     def share(layer, first, adjoint):
         for part in range(2):
@@ -294,71 +300,34 @@
                 term = lambda m: first[m, 0] * adjoint[m, 1] - first[m, 1] * adjoint[m, 0]
             grad = (term(0) + term(1)).astype(BF)
             gsend[layer, part] = dot(dot(turn_rows, grad).astype(BF), turn_cols).astype(BF)
-        start(pair(layer))
+        wins[layer, s] = gsend[layer, core]
+
+    def launch(j):
         for c in range(2):
-            start(near(layer, c, 1))
-            start(near(layer, c, 0))
-        wins[layer, s] = gsend[layer, core]
-
-    def pass_on(layer):
-        for side in (1, 0):
-            for c in range(2):
-                near_in(layer, c, side).wait_recv()
-                start(relay(layer, c, side))
-
-    share(1, arr, cur)
-
-    def behind(rows, i):
-        re, im = win[1, 0, rows, :], win[1, 1, rows, :]
-        for m in range(2):
-            cr, ci = cur[m, 0, rows, :], cur[m, 1, rows, :]
-            put(m, rows, i, re * cr + im * ci, re * ci - im * cr)
-
-    by_rows(behind)
-    left_mul(e_c)
-    right_mul(e_h, cur)
-    share(0, probe, cur)
-
-    def leave(rows, i):
-        re, im = win[0, 0, rows, :], win[0, 1, rows, :]
-        for m in range(2):
-            cr, ci = cur[m, 0, rows, :], cur[m, 1, rows, :]
-            esend[m, 0, rows, :] = (re * cr + im * ci).astype(BF)
-            esend[m, 1, rows, :] = (re * ci - im * cr).astype(BF)
-
-    by_rows(leave)
-    q_pair, q_y, q_z, q_x = 53, 54, 57, 64
-    e_copy = remote(esend.at[other], erecv, send.at[q_pair], recv.at[q_pair], (partner, o))
-    start(e_copy)
-    pass_on(1)
-    e_copy.wait_recv()
-
-    def add_pair(rows, i):
-        for part in range(2):
-            ysend[part, rows, :] = (esend[core, part, rows, :].astype(F32) + erecv[part, rows, :].astype(F32)).astype(BF)
-
-    by_rows(add_pair)
-    deep = N // NY
-    y_copies = []
-    for k in range(1, NY):
-        y_to = rem(y + k, NY)
-        rows_to = pl.ds(pl.multiple_of(y_to * deep, deep), deep)
-        copy = remote(
-            ysend.at[:, rows_to, :], yrecv.at[k - 1], send.at[q_y + k - 1], recv.at[q_y + k - 1], (s, y_to * NZ + z)
-        )
-        start(copy)
-        y_copies.append(copy)
+            start(near(j, c, 1))
+            start(near(j, c, 0))
+        start(pair(j))
+
+    def pass_on(j):
+        for c in range(2):
+            for side in (1, 0):
+                near_in(j, c, side).wait_recv()
+                start(relay(j, c, side))
 
     lane = lax.broadcasted_iota(jnp.int32, (1, N), 1)
-
-    def gather(layer):
+    cols = [
+        [jnp.where((lane + (2 * x + b) * N >= c0) & (lane + (2 * x + b) * N < c0 + N), 1.0, 0.0) for b in range(2)]
+        for _, _, c0 in places
+    ]
+
+    def gather(j):
+        layer, first = chunks[j][0], chunks[j][1] * half
         chunk = 16
-        cols = [[(lane + (2 * x + b) * N >= c0) & (lane + (2 * x + b) * N < c0 + N) for b in range(2)] for _, _, c0 in places]
-        cols = [[jnp.where(mask, 1.0, 0.0).astype(F32) for mask in pair_masks] for pair_masks in cols]
 
         def run(i, carry):
-            rows = pl.ds(pl.multiple_of(i * chunk, chunk), chunk)
-            line = lax.broadcasted_iota(jnp.int32, (chunk, N), 0) + i * chunk
+            at = pl.multiple_of(first + i * chunk, chunk)
+            rows = pl.ds(at, chunk)
+            line = lax.broadcasted_iota(jnp.int32, (chunk, N), 0) + at
             sums = [[jnp.zeros((chunk, N), F32) for _ in range(2)] for _ in range(2)]
             for n in range(NS):
                 term = wins[layer, n, rows, :].astype(F32)
@@ -374,86 +343,141 @@
                 bsend[layer, b, rows, :] = sums[b][1].astype(BF)
             return carry
 
-        lax.fori_loop(0, N // chunk, run, 0)
-
-    def top_copy(layer):
-        q = 71 + layer
-        return remote(tsend.at[layer], trecv.at[layer], send.at[q], recv.at[q], (partner, o))
-
-    def bottom_copy(layer, b):
-        q = 73 + 2 * layer
-        return remote(bsend.at[layer, b], brecv.at[layer, core], send.at[q + b], recv.at[q + core], (2 * x + b, up))
-
-    def bottom_in(layer, c):
-        q = 73 + 2 * layer
-        return remote(bsend.at[layer, c], brecv.at[layer, c], send.at[q + c], recv.at[q + c], (s, up))
-
-    def collect(layer):
-        pair(layer, True).wait_recv()
-        for side in (1, 0):
-            for c in range(2):
-                relay(layer, c, side, True).wait_recv()
-        gather(layer)
+        lax.fori_loop(0, half // chunk, run, 0)
+
+    def top_copy(j):
+        layer, q = chunks[j][0], 21 + 14 * j
+        return remote(tsend.at[layer, span(j)], trecv.at[layer, span(j)], send.at[q], recv.at[q], (partner, o))
+
+    def bottom_copy(j, b):
+        layer, q = chunks[j][0], 22 + 14 * j
+        return remote(
+            bsend.at[layer, b, span(j)], brecv.at[layer, core, span(j)], send.at[q + b], recv.at[q + core], (2 * x + b, up)
+        )
+
+    def bottom_in(j, c):
+        layer, q = chunks[j][0], 22 + 14 * j
+        return remote(bsend.at[layer, c, span(j)], brecv.at[layer, c, span(j)], send.at[q + c], recv.at[q + c], (s, up))
+
+    def collect(j):
+        pair(j, True).wait_recv()
+        for c in range(2):
+            for side in (1, 0):
+                relay(j, c, side, True).wait_recv()
+        gather(j)
         for b in range(2):
-            start(bottom_copy(layer, b))
-        start(top_copy(layer))
-
-    def finish(layer):
-        top_copy(layer).wait_recv()
+            start(bottom_copy(j, b))
+        start(top_copy(j))
+
+    def finish(j):
+        layer = chunks[j][0]
+        top_copy(j).wait_recv()
         for c in range(2):
-            bottom_in(layer, c).wait_recv()
-        for i in range(N // 64):
-            rows = pl.ds(i * 64, 64)
+            bottom_in(j, c).wait_recv()
+        for i in range(2):
+            rows = span(j, i)
             out_ref[layer, core, rows, :] = acc[layer, rows, :] + brecv[layer, core, rows, :].astype(F32)
             out_ref[layer, other, rows, :] = (
                 trecv[layer, rows, :].astype(F32) + brecv[layer, other, rows, :].astype(F32)
             )
 
-    collect(1)
+    share(1, arr, cur)
+    launch(0)
+    launch(1)
+
+    def behind(rows, i):
+        re, im = win[1, 0, rows, :], win[1, 1, rows, :]
+        for m in range(2):
+            cr, ci = cur[m, 0, rows, :], cur[m, 1, rows, :]
+            put(m, rows, i, re * cr + im * ci, re * ci - im * cr)
+
+    by_rows(behind)
+    left_mul(e_c)
+    right_mul(e_h, cur)
+
+    def leave(rows, i):
+        re, im = win[0, 0, rows, :], win[0, 1, rows, :]
+        for m in range(2):
+            cr, ci = cur[m, 0, rows, :], cur[m, 1, rows, :]
+            esend[m, 0, rows, :] = (re * cr + im * ci).astype(BF)
+            esend[m, 1, rows, :] = (re * ci - im * cr).astype(BF)
+
+    by_rows(leave)
+    q_pair, q_y, q_z, q_x = 67, 68, 71, 78
+    e_copy = remote(esend.at[other], erecv, send.at[q_pair], recv.at[q_pair], (partner, o))
+    start(e_copy)
+    share(0, probe, cur)
+    e_copy.wait_recv()
+
+    def add_pair(rows, i):
+        for part in range(2):
+            ysend[part, rows, :] = (esend[core, part, rows, :].astype(F32) + erecv[part, rows, :].astype(F32)).astype(BF)
+
+    by_rows(add_pair)
+    deep = N // NY
+    y_copies = []
+    for k in range(1, NY):
+        y_to = rem(y + k, NY)
+        rows_to = pl.ds(pl.multiple_of(y_to * deep, deep), deep)
+        copy = remote(
+            ysend.at[:, rows_to, :], yrecv.at[k - 1], send.at[q_y + k - 1], recv.at[q_y + k - 1], (s, y_to * NZ + z)
+        )
+        start(copy)
+        y_copies.append(copy)
+    pass_on(0)
+    launch(2)
     for copy in y_copies:
         copy.wait_recv()
     rows_me = pl.ds(pl.multiple_of(y * deep, deep), deep)
+    totals = []
     for part in range(2):
         total = ysend[part, rows_me, :].astype(F32)
         for k in range(NY - 1):
             total = total + yrecv[k, part].astype(F32)
-        zsend[part] = total
+        totals.append(total)
+    for k in range(NZ):
+        zsend[k] = jnp.concatenate([total[8 * k : 8 * k + 8] for total in totals], axis=0).astype(BF)
     z_copies = []
     for k in range(1, NZ):
         z_to = rem(z + k, NZ)
         copy = remote(
-            zsend.at[:, pl.ds(pl.multiple_of(z_to * 8, 8), 8), :], zrecv.at[k - 1],
-            send.at[q_z + k - 1], recv.at[q_z + k - 1], (s, y * NZ + z_to),
+            zsend.at[z_to], zrecv.at[k - 1], send.at[q_z + k - 1], recv.at[q_z + k - 1], (s, y * NZ + z_to)
         )
         start(copy)
         z_copies.append(copy)
-    pass_on(0)
+    pass_on(1)
+    launch(3)
+    collect(0)
     for copy in z_copies:
         copy.wait_recv()
-    for part in range(2):
-        total = zsend[part, pl.ds(pl.multiple_of(z * 8, 8), 8), :]
-        for k in range(NZ - 1):
-            total = total + zrecv[k, part]
-        xsend[part] = total
+    total = zsend[z].astype(F32)
+    for k in range(NZ - 1):
+        total = total + zrecv[k].astype(F32)
+    xall[0] = total.astype(BF)
     x_copies = []
     for k in range(1, NS):
-        copy = remote(xsend, xrecv.at[k - 1], send.at[q_x + k - 1], recv.at[q_x + k - 1], (rem(s + k, NS), o))
+        copy = remote(xall.at[0], xall.at[k], send.at[q_x + k - 1], recv.at[q_x + k - 1], (rem(s + k, NS), o))
         start(copy)
         x_copies.append(copy)
-    collect(0)
+    pass_on(2)
+    collect(1)
+    pass_on(3)
+    finish(0)
+    collect(2)
     for copy in x_copies:
         copy.wait_recv()
+    pick = one_hot((N, 128), lambda a, b: a == b + 32 * s)
     factor = 1.0 / math.sqrt(256.0)
-    mine, theirs = xsend[...], xrecv[0]
-    for k in range(2, NS):
-        if k % 2:
-            theirs = theirs + xrecv[k - 1]
-        else:
-            mine = mine + xrecv[k - 1]
-    pout_ref[core] = mine * factor
-    pout_ref[other] = theirs * factor
+    shares = [dot(xall[k], pick) for k in range(NS)]
+    mine = (shares[0] + shares[2] + (shares[4] + shares[6])) * factor
+    theirs = (shares[1] + shares[3] + (shares[5] + shares[7])) * factor
+    for part in range(2):
+        pout_ref[core, part] = mine[8 * part : 8 * part + 8, :32]
+        pout_ref[other, part] = theirs[8 * part : 8 * part + 8, :32]
     finish(1)
-    finish(0)
+    collect(3)
+    finish(2)
+    finish(3)
     for copy in sends:
         copy.wait_send()
 
@@ -462,11 +486,11 @@
     vmem = pltpu.VMEM
     square = lambda *lead: (*lead, N, N)
     any_spec = pl.BlockSpec(memory_space=pl.ANY)
-    object_grad, probe_rows = pl.pallas_call(
+    return pl.pallas_call(
         main_kernel,
         out_shape=(
             jax.ShapeDtypeStruct(square(2, 2), F32),
-            jax.ShapeDtypeStruct((2, 2, 8, N), F32),
+            jax.ShapeDtypeStruct((2, 2, 8, 32), F32),
         ),
         in_specs=[pl.BlockSpec(memory_space=pltpu.SMEM)] * 2 + [any_spec] * 4,
         out_specs=(pl.BlockSpec(memory_space=vmem), pl.BlockSpec(memory_space=vmem)),
@@ -500,21 +524,18 @@
             vmem(square(2), BF),
             vmem(square(2), BF),
             vmem((NY - 1, 2, N // NY, N), BF),
-            vmem((2, N // NY, N), F32),
-            vmem((NZ - 1, 2, 8, N), F32),
-            vmem((2, 8, N), F32),
-            vmem((NS - 1, 2, 8, N), F32),
+            vmem((NZ, 16, N), BF),
+            vmem((NZ - 1, 16, N), BF),
+            vmem((NS, 16, N), BF),
             pltpu.SemaphoreType.DMA((4 + 2 * NS,)),
-            pltpu.SemaphoreType.DMA((93,)),
-            pltpu.SemaphoreType.DMA((93,)),
+            pltpu.SemaphoreType.DMA((101,)),
+            pltpu.SemaphoreType.DMA((101,)),
         ],
         compiler_params=pltpu.CompilerParams(
             collective_id=0, has_side_effects=True, vmem_limit_bytes=60 * 1024 * 1024
         ),
         name="gradient",
     )(positions[0, 0], counts, object_slices, probe, measured[0, 0], tables())
-    cols = lax.axis_index("scan") * 32
-    return object_grad, lax.dynamic_slice_in_dim(probe_rows, cols, 32, axis=3)
 
 
 def solution(mesh):

time: 78.9 us -> 72 us (0.913)
  Pallas kernels: 73.7 us -> 66.9 us
    pallas_call x1, Pallas kernels: 73.7 us -> 66.9 us  [body(): pl.pallas_call(main_kernel, out_shape=(jax.ShapeDtypeStruct(square(2, 2),...]
    dynamic_slice x1 -> x0, local copies, waits for them, and re-layouts: 1.4 us -> none  [body(): return (object_grad, lax.dynamic_slice_in_dim(probe_rows, cols, 32, axis=3))]
    unnamed x1 -> x2, local copies, waits for them, and re-layouts: 2.28 us -> 3.61 us
where the time goes in v3:
time: 72 us; the launch traced here: 71.8 us
  Pallas kernels  66.9 us (93%)
  local copies, waits for them, and re-layouts  3.61 us (5%)
  between operations  1.29 us (2%)
    pallas_call x1, Pallas kernels, body(): pl.pallas_call(main_kernel, out_shape=(jax.ShapeDtypeStruct(square(2, 2),...  66.9 us
    unnamed x2, local copies, waits for them, and re-layouts  3.61 us

profile of v3, /device:TPU:1, one launch (start us, length us, event | category | flops | bytes accessed | tf_op | source)
XLA Modules:
  0.0 71.8 jit_solution(7315321103868504315)
XLA Ops:
  1.3 66.9 %gradient.1 = (f32[2,2,256,256]{3,2,1,0:T(8,128)}, f32[2,2,8,32]{3,2,1,0:T(8,128)}) custom-call(s32[2,2]{1,0:T(2,128)} %bitcast.3, s32[1,1]{1,0:T(1,128)S(6)} %copy.10.count_ref, f32[2,2,256,2048]{3,2,1,0:T(8,128)} %tile_hbm.1, f32[2,2,256,256]{3,2,1,0:T(8,128)} %probe_hbm.1, bf16[2,256,256]{2,1,0:T(8,128)(2,1)} %bitcast.2, ...), custom_call_target="tpu_custom_call" | custom-call | tf_op jit(solution)/shard_map/gradient/pallas_call | solution.py:489
  68.2 2.3 %copy.11 = f32[2,2,256,256]{3,2,1,0:T(8,128)} copy(f32[2,2,256,256]{3,2,1,0:T(8,128)} %get-tuple-element.4) | data formatting | bytes 2097152
  70.5 1.3 %copy.12 = f32[2,2,8,32]{3,2,1,0:T(8,128)} copy(f32[2,2,8,32]{3,2,1,0:T(8,128)} %get-tuple-element.5) | data formatting | bytes 8192

commit v4 on v3

--- a/solution.py
+++ b/solution.py
@@ -39,9 +39,9 @@
 
 
 def main_kernel(
-    pos_ref, count_ref, tile_hbm, probe_hbm, meas_hbm, table_hbm, out_ref, pout_ref,
-    row, rows_in, tab, tile_0, tile_1, probe, meas, tabs, e_f, e_i, e_h, e_c, hsend, hrecv, local, pattern, win, v, u, arr, far, cur,
-    gsend, wins, acc, tsend, trecv, bsend, brecv, esend, erecv, ysend, yrecv, zsend, zrecv, xall,
+    count_ref, pos_hbm, tile_hbm, probe_hbm, meas_hbm, table_hbm, out_hbm, pout_ref,
+    pos_ref, row, rows_in, tab, tile_0, tile_1, probe, meas, tabs, e_f, e_i, e_h, e_c, hsend, hrecv, local, pattern, win, v, u, arr, far, cur,
+    gsend, wins, acc, done, tsend, trecv, bsend, brecv, esend, erecv, ysend, yrecv, zsend, zrecv, xall,
     dma, send, recv,
 ):
     s, o = lax.axis_index("scan"), lax.axis_index("obj")
@@ -58,7 +58,7 @@
     far_at = [2 * rem(x + 2, NX) + c for c in range(2)]
     up, down = rem(o + 1, NO), rem(o + NO - 1, NO)
     tile = (tile_0, tile_1)
-    sends = []
+    sends, gone = [], []
 
     barrier = pltpu.get_barrier_semaphore()
     peers = [(rem(s + k, NS), o) for k in range(1, NS)]
@@ -68,6 +68,8 @@
     for peer in peers:
         pl.semaphore_signal(barrier, inc=1, device_id=peer, device_id_type=MESH)
 
+    given = pltpu.make_async_copy(pos_hbm, pos_ref, dma.at[4 + 2 * NS])
+    given.start()
     loads = [
         pltpu.make_async_copy(table_hbm, tabs, dma.at[0]),
         pltpu.make_async_copy(probe_hbm, probe, dma.at[1]),
@@ -81,12 +83,53 @@
         load.start()
 
     lane = lax.broadcasted_iota(jnp.int32, (1, 128), 1)
+    given.wait()
     line = jnp.zeros((1, 128), jnp.int32)
     for j, value in enumerate((pos_ref[0, 0], pos_ref[0, 1], pos_ref[1, 0], pos_ref[1, 1], count_ref[0, 0])):
         line = jnp.where(lane == j, value, line)
     row[...] = line
     rows_in[s] = line
 
+    def one_hot(shape, rule):
+        a, b = lax.broadcasted_iota(jnp.int32, shape, 0), lax.broadcasted_iota(jnp.int32, shape, 1)
+        return jnp.where(rule(a, b), 1.0, 0.0).astype(BF)
+
+    def dot(a, b):
+        return jnp.dot(a, b, preferred_element_type=F32)
+
+    def col_block(col):
+        k = jnp.int32(0)
+        for edge in range(1, NS - 1):
+            k = k + jnp.where(col >= edge * N, 1, 0)
+        return k
+
+    def picks(offset):
+        return [one_hot((N, N), lambda a, b: a + h * N == b + offset) for h in range(2)]
+
+    def columns(layer, part, k, pick):
+        first, second = tile[layer][k, part].astype(BF), tile[layer][k + 1, part].astype(BF)
+        return (dot(first, pick[0]) + dot(second, pick[1])).astype(BF)
+
+
+    pl.semaphore_wait(barrier, len(peers))
+
+    def start(copy):
+        copy.start()
+        sends.append(copy)
+
+    def meas_copy(q, slot, n, peer):
+        ref = meas.at[pl.ds(slot, n)]
+        return remote(ref, ref, send.at[q], recv.at[q], (peer, o))
+
+    def place_copy(k, base, owner):
+        peer = (rem(s + k, NS), up if base else o)
+        return remote(row, rows_in.at[base + owner], send.at[85 + base + k], recv.at[85 + base + k], peer)
+
+    every = [(k, base) for base in (0, NS) for k in range(NS) if base or k]
+    for k, base in every:
+        start(place_copy(k, base, s))
+    for q, peer in ((0, partner), (1, right_me), (2, left_me)):
+        start(remote(meas_hbm, meas.at[pl.ds(2 * s, 2)], send.at[q], recv.at[q], (peer, o)))
     loads[0].wait()
     for e_ref, re, im, sign in ((e_f, 0, 1, 1), (e_i, 0, 1, -1), (e_h, 2, 3, 1), (e_c, 2, 3, -1)):
         e_ref[0:N, 0:N] = tabs[re]
@@ -94,50 +137,10 @@
         e_ref[0:N, N:] = -tabs[im] if sign > 0 else tabs[im]
         e_ref[N:, 0:N] = tabs[im] if sign > 0 else -tabs[im]
 
-    def one_hot(shape, rule):
-        a, b = lax.broadcasted_iota(jnp.int32, shape, 0), lax.broadcasted_iota(jnp.int32, shape, 1)
-        return jnp.where(rule(a, b), 1.0, 0.0).astype(BF)
-
-    def dot(a, b):
-        return jnp.dot(a, b, preferred_element_type=F32)
-
-    def col_block(col):
-        k = jnp.int32(0)
-        for edge in range(1, NS - 1):
-            k = k + jnp.where(col >= edge * N, 1, 0)
-        return k
-
-    def picks(offset):
-        return [one_hot((N, N), lambda a, b: a + h * N == b + offset) for h in range(2)]
-
-    def columns(layer, part, k, pick):
-        first, second = tile[layer][k, part].astype(BF), tile[layer][k + 1, part].astype(BF)
-        return (dot(first, pick[0]) + dot(second, pick[1])).astype(BF)
-
-
-    pl.semaphore_wait(barrier, len(peers))
-
-    def start(copy):
-        copy.start()
-        sends.append(copy)
-
-    def meas_copy(q, slot, n, peer):
-        ref = meas.at[pl.ds(slot, n)]
-        return remote(ref, ref, send.at[q], recv.at[q], (peer, o))
-
-    def place_copy(k, base, owner):
-        peer = (rem(s + k, NS), up if base else o)
-        return remote(row, rows_in.at[base + owner], send.at[85 + base + k], recv.at[85 + base + k], peer)
-
-    every = [(k, base) for base in (0, NS) for k in range(NS) if base or k]
-    for k, base in every:
-        start(place_copy(k, base, s))
     for k, base in every:
         place_copy(k, base, rem(s + NS - k, NS)).wait_recv()
     fetch = pltpu.make_async_copy(rows_in, tab, dma.at[3 + 2 * NS])
     fetch.start()
-    for q, peer in ((0, partner), (1, right_me), (2, left_me)):
-        start(remote(meas_hbm, meas.at[pl.ds(2 * s, 2)], send.at[q], recv.at[q], (peer, o)))
     fetch.wait()
 
     def assigned(base, n):
@@ -376,10 +379,15 @@
             bottom_in(j, c).wait_recv()
         for i in range(2):
             rows = span(j, i)
-            out_ref[layer, core, rows, :] = acc[layer, rows, :] + brecv[layer, core, rows, :].astype(F32)
-            out_ref[layer, other, rows, :] = (
+            done[layer, core, rows, :] = acc[layer, rows, :] + brecv[layer, core, rows, :].astype(F32)
+            done[layer, other, rows, :] = (
                 trecv[layer, rows, :].astype(F32) + brecv[layer, other, rows, :].astype(F32)
             )
+        leaving = pltpu.make_async_copy(
+            done.at[layer, :, span(j)], out_hbm.at[layer, :, span(j)], dma.at[6 + 2 * NS + j]
+        )
+        leaving.start()
+        gone.append(leaving)
 
     share(1, arr, cur)
     launch(0)
@@ -426,6 +434,8 @@
         y_copies.append(copy)
     pass_on(0)
     launch(2)
+    pass_on(1)
+    launch(3)
     for copy in y_copies:
         copy.wait_recv()
     rows_me = pl.ds(pl.multiple_of(y * deep, deep), deep)
@@ -445,9 +455,9 @@
         )
         start(copy)
         z_copies.append(copy)
-    pass_on(1)
-    launch(3)
     collect(0)
+    pass_on(2)
+    collect(1)
     for copy in z_copies:
         copy.wait_recv()
     total = zsend[z].astype(F32)
@@ -459,8 +469,6 @@
         copy = remote(xall.at[0], xall.at[k], send.at[q_x + k - 1], recv.at[q_x + k - 1], (rem(s + k, NS), o))
         start(copy)
         x_copies.append(copy)
-    pass_on(2)
-    collect(1)
     pass_on(3)
     finish(0)
     collect(2)
@@ -478,23 +486,31 @@
     collect(3)
     finish(2)
     finish(3)
+    for copy in gone:
+        copy.wait()
     for copy in sends:
         copy.wait_send()
+
+
+def hand_on(grad_ref, probe_ref, grad_out, probe_out):
+    grad_out[...] = grad_ref[...]
+    probe_out[...] = probe_ref[...]
 
 
 def body(object_slices, probe, measured, positions, counts):
     vmem = pltpu.VMEM
     square = lambda *lead: (*lead, N, N)
     any_spec = pl.BlockSpec(memory_space=pl.ANY)
-    return pl.pallas_call(
+    results = pl.pallas_call(
         main_kernel,
         out_shape=(
             jax.ShapeDtypeStruct(square(2, 2), F32),
             jax.ShapeDtypeStruct((2, 2, 8, 32), F32),
         ),
-        in_specs=[pl.BlockSpec(memory_space=pltpu.SMEM)] * 2 + [any_spec] * 4,
-        out_specs=(pl.BlockSpec(memory_space=vmem), pl.BlockSpec(memory_space=vmem)),
+        in_specs=[pl.BlockSpec(memory_space=pltpu.SMEM)] + [any_spec] * 5,
+        out_specs=(any_spec, pl.BlockSpec(memory_space=vmem)),
         scratch_shapes=[
+            pltpu.SMEM((2, 2), jnp.int32),
             vmem((1, 128), jnp.int32),
             vmem((2 * NS, 1, 128), jnp.int32),
             pltpu.SMEM((2 * NS, 1, 128), jnp.int32),
@@ -516,6 +532,7 @@
             vmem(square(2, 2), BF),
             vmem(square(2, NS), BF),
             vmem(square(2), F32),
+            vmem(square(2, 2), F32),
             vmem(square(2), BF),
             vmem(square(2), BF),
             vmem(square(2, 2), BF),
@@ -527,7 +544,7 @@
             vmem((NZ, 16, N), BF),
             vmem((NZ - 1, 16, N), BF),
             vmem((NS, 16, N), BF),
-            pltpu.SemaphoreType.DMA((4 + 2 * NS,)),
+            pltpu.SemaphoreType.DMA((10 + 2 * NS,)),
             pltpu.SemaphoreType.DMA((101,)),
             pltpu.SemaphoreType.DMA((101,)),
         ],
@@ -535,7 +552,17 @@
             collective_id=0, has_side_effects=True, vmem_limit_bytes=60 * 1024 * 1024
         ),
         name="gradient",
-    )(positions[0, 0], counts, object_slices, probe, measured[0, 0], tables())
+    )(counts, positions[0, 0], object_slices, probe, measured[0, 0], tables())
+    plane = pl.BlockSpec((1, 1, N, N), lambda a, b: (a, b, 0, 0))
+    whole = pl.BlockSpec((2, 2, 8, 32), lambda a, b: (0, 0, 0, 0))
+    return pl.pallas_call(
+        hand_on,
+        out_shape=tuple(jax.ShapeDtypeStruct(r.shape, F32) for r in results),
+        grid=(2, 2),
+        in_specs=[plane, whole],
+        out_specs=(plane, whole),
+        name="results",
+    )(*results)
 
 
 def solution(mesh):

time: 72 us -> 70.9 us (0.985)
  local copies, waits for them, and re-layouts: 3.61 us -> 0 us
  Pallas kernels: 66.9 us -> 69.5 us
    unnamed x2 -> x0, local copies, waits for them, and re-layouts: 3.61 us -> none
    pallas_call x0 -> x1, Pallas kernels: none -> 3.38 us  [body(): pl.pallas_call(hand_on, out_shape=tuple((jax.ShapeDtypeStruct(r.shape, F3...]
    pallas_call x1, Pallas kernels: 66.9 us -> 66.1 us  [body(): pl.pallas_call(main_kernel, out_shape=(jax.ShapeDtypeStruct(square(2, 2),...]
where the time goes in v4:
time: 70.9 us; the launch traced here: 70.8 us
  Pallas kernels  69.5 us (98%)
  between operations  1.29 us (2%)
    pallas_call x1, Pallas kernels, body(): pl.pallas_call(main_kernel, out_shape=(jax.ShapeDtypeStruct(square(2, 2),...  66.1 us
    pallas_call x1, Pallas kernels, body(): pl.pallas_call(hand_on, out_shape=tuple((jax.ShapeDtypeStruct(r.shape, F3...  3.38 us

profile of v4, /device:TPU:1, one launch (start us, length us, event | category | flops | bytes accessed | tf_op | source)
XLA Modules:
  0.0 70.8 jit_solution(106921717607525206)
XLA Ops:
  1.3 66.1 %gradient.1 = (f32[2,2,256,256]{3,2,1,0:T(8,128)}, f32[2,2,8,32]{3,2,1,0:T(8,128)}) custom-call(s32[1,1]{1,0:T(1,128)S(6)} %copy.8.count_ref, s32[2,2]{1,0:T(2,128)} %bitcast.3, f32[2,2,256,2048]{3,2,1,0:T(8,128)} %tile_hbm.1, f32[2,2,256,256]{3,2,1,0:T(8,128)} %probe_hbm.1, bf16[2,256,256]{2,1,0:T(8,128)(2,1)} %bitcast.2, ...), custom_call_target="tpu_custom_call" | custom-call | tf_op jit(solution)/shard_map/gradient/pallas_call | solution.py:504
  67.4 3.4 %results.1 = (f32[2,2,256,256]{3,2,1,0:T(8,128)}, f32[2,2,8,32]{3,2,1,0:T(8,128)}) custom-call(f32[2,2,256,256]{3,2,1,0:T(8,128)} %get-tuple-element.4.grad_ref, f32[2,2,8,32]{3,2,1,0:T(8,128)} %get-tuple-element.5.probe_ref), custom_call_target="tpu_custom_call" | custom-call | tf_op jit(solution)/shard_map/results/pallas_call | solution.py:558

commit v5 on v4

--- a/solution.py
+++ b/solution.py
@@ -40,8 +40,8 @@
 
 def main_kernel(
     count_ref, pos_hbm, tile_hbm, probe_hbm, meas_hbm, table_hbm, out_hbm, pout_ref,
-    pos_ref, row, rows_in, tab, tile_0, tile_1, probe, meas, tabs, e_f, e_i, e_h, e_c, hsend, hrecv, local, pattern, win, v, u, arr, far, cur,
-    gsend, wins, acc, done, tsend, trecv, bsend, brecv, esend, erecv, ysend, yrecv, zsend, zrecv, xall,
+    pos_ref, row, rows_in, tab, tile_0, tile_1, probe, meas, tabs, e_f, e_i, e_h, e_c, hsend, hrecv, local, offer, offered, chosen, pattern, win, v, u, arr, far, cur,
+    gsend, wins, acc, done, tsend, trecv, bsend, brecv, csend, crecv, esend, erecv, ysend, yrecv, zsend, zrecv, xall,
     dma, send, recv,
 ):
     s, o = lax.axis_index("scan"), lax.axis_index("obj")
@@ -52,9 +52,7 @@
     right = [2 * rem(x + 1, NX) + c for c in range(2)]
     left = [2 * rem(x + 3, NX) + c for c in range(2)]
     right_me, left_me = 2 * rem(x + 1, NX) + core, 2 * rem(x + 3, NX) + core
-    far_me, left_ot, right_ot, far_ot = (
-        2 * rem(x + 2, NX) + core, 2 * rem(x + 3, NX) + other, 2 * rem(x + 1, NX) + other, 2 * rem(x + 2, NX) + other
-    )
+    x_left, x_right, x_far = rem(x + 3, NX), rem(x + 1, NX), rem(x + 2, NX)
     far_at = [2 * rem(x + 2, NX) + c for c in range(2)]
     up, down = rem(o + 1, NO), rem(o + NO - 1, NO)
     tile = (tile_0, tile_1)
@@ -62,7 +60,7 @@
 
     barrier = pltpu.get_barrier_semaphore()
     peers = [(rem(s + k, NS), o) for k in range(1, NS)]
-    peers += [(s, up)] + [(rem(s + k, NS), down) for k in range(NS)]
+    peers += [(s, up), (partner, up)] + [(rem(s + k, NS), down) for k in range(NS)]
     peers += [(s, rem(y + k, NY) * NZ + z) for k in range(1, NY)]
     peers += [(s, y * NZ + rem(z + k, NZ)) for k in range(1, NZ)]
     for peer in peers:
@@ -73,7 +71,7 @@
     loads = [
         pltpu.make_async_copy(table_hbm, tabs, dma.at[0]),
         pltpu.make_async_copy(probe_hbm, probe, dma.at[1]),
-        pltpu.make_async_copy(meas_hbm, meas.at[pl.ds(2 * s, 2)], dma.at[2]),
+        pltpu.make_async_copy(meas_hbm, meas.at[pl.ds(2 * x, 2)], dma.at[2]),
     ]
     for layer in range(2):
         for b in range(NS):
@@ -123,13 +121,13 @@
 
     def place_copy(k, base, owner):
         peer = (rem(s + k, NS), up if base else o)
-        return remote(row, rows_in.at[base + owner], send.at[85 + base + k], recv.at[85 + base + k], peer)
+        return remote(row, rows_in.at[base + owner], send.at[93 + base + k], recv.at[93 + base + k], peer)
 
     every = [(k, base) for base in (0, NS) for k in range(NS) if base or k]
     for k, base in every:
         start(place_copy(k, base, s))
-    for q, peer in ((0, partner), (1, right_me), (2, left_me)):
-        start(remote(meas_hbm, meas.at[pl.ds(2 * s, 2)], send.at[q], recv.at[q], (peer, o)))
+    for q, peer in ((1, right_me), (2, left_me)):
+        start(remote(meas_hbm, meas.at[pl.ds(2 * x, 2)], send.at[q], recv.at[q], (peer, o)))
     loads[0].wait()
     for e_ref, re, im, sign in ((e_f, 0, 1, 1), (e_i, 0, 1, -1), (e_h, 2, 3, 1), (e_c, 2, 3, -1)):
         e_ref[0:N, 0:N] = tabs[re]
@@ -144,40 +142,42 @@
     fetch.wait()
 
     def assigned(base, n):
-        start, found = jnp.int32(0), [jnp.int32(0)] * 3
+        begin, found = jnp.int32(0), [jnp.int32(0)] * 4
         for t in range(NS):
             count = tab[base + t, 0, 4]
             for k in range(2):
-                hit = (k < count) & (start + k == n)
-                for j, value in enumerate((jnp.int32(2 * t + k), tab[base + t, 0, 2 * k], tab[base + t, 0, 2 * k + 1])):
+                hit = (k < count) & (begin + k == n)
+                values = (jnp.int32(t % 2), jnp.int32(2 * (t // 2) + k), tab[base + t, 0, 2 * k], tab[base + t, 0, 2 * k + 1])
+                for j, value in enumerate(values):
                     found[j] = jnp.where(hit, value, found[j])
-            start = start + count
+            begin = begin + count
         return found
 
-    places = [assigned(0, n) for n in range(NS)]
-    source, row0, col0 = places[0]
-    for n in range(1, NS):
-        source, row0, col0 = (jnp.where(s == n, a, b) for a, b in zip(places[n], (source, row0, col0)))
-    _, _, col_prev = assigned(NS, s)
-
-    k_prev, k_own = col_block(col_prev), col_block(col0)
-    pick_prev = picks(col_prev - k_prev * N)
+    _, _, _, col_out = assigned(NS * other, x + NX * core)
+    k_out = col_block(col_out)
+    pick_out = picks(col_out - k_out * N)
+    halo_to = jnp.where(core == 0, down, up)
 
     def halo_copy(layer):
-        return remote(hsend.at[layer], hrecv.at[layer], send.at[9 + layer], recv.at[9 + layer], (s, down))
+        return remote(hsend.at[layer], hrecv.at[layer], send.at[9 + layer], recv.at[9 + layer], (s, halo_to))
 
     for layer in range(2):
         for b in range(NS):
             loads[3 + NS * layer + b].wait()
         for part in range(2):
-            hsend[layer, part] = columns(layer, part, k_prev, pick_prev)
+            hsend[layer, part] = columns(layer, part, k_out, pick_out)
         start(halo_copy(layer))
+    _, _, row0, col0 = assigned(NS * core, x + NX * core)
+    k_own = col_block(col0)
     pick_own = picks(col0 - k_own * N)
     for layer in range(2):
         for part in range(2):
             local[layer, part] = columns(layer, part, k_own, pick_own)
-    rows_here = one_hot((N, N), lambda a, b: b == a + row0)
-    rows_next = one_hot((N, N), lambda a, b: b + N == a + row0)
+    places = [assigned(NS * (d % 2), d // 2 + NX * (d % 2))[2:] for d in range(NS)]
+    half_has, slot_has, _, _ = assigned(0, x + NX * core)
+    _, slot_other, _, _ = assigned(0, x + NX * other)
+    rows_own = one_hot((N, N), lambda a, b: b + N * core == a + row0)
+    rows_halo = one_hot((N, N), lambda a, b: b + N * other == a + row0)
     turn = jnp.where(col0 == 7 * N, 0, col0 - k_own * N)
     turn_rows = one_hot((N, N), lambda a, b: (b + row0 == a) | (b + row0 == a + N))
     turn_cols = one_hot((N, N), lambda a, b: (a + turn == b) | (a + turn == b + N))
@@ -186,7 +186,7 @@
     def window(layer):
         halo_copy(layer).wait_recv()
         for part in range(2):
-            win[layer, part] = dot(rows_here, local[layer, part]) + dot(rows_next, hrecv[layer, part])
+            win[layer, part] = dot(rows_own, local[layer, part]) + dot(rows_halo, hrecv[layer, part])
 
     step = 32
 
@@ -213,6 +213,11 @@
             result[0, part] = product[0:N]
             result[1, part] = product[N:]
 
+    meas_copy(1, 2 * x_left, 2, right_me).wait_recv()
+    start(meas_copy(3, 2 * x_left, 1, right_me))
+    meas_copy(2, 2 * x_right, 2, left_me).wait_recv()
+    start(meas_copy(5, 2 * x_right + 1, 1, left_me))
+
     window(0)
 
     def enter(rows, i):
@@ -222,14 +227,22 @@
             put(m, rows, i, pr * re - pi * im, pr * im + pi * re)
 
     by_rows(enter)
+    meas_copy(3, 2 * x_far, 1, right_me).wait_recv()
+    meas_copy(5, 2 * x_far + 1, 1, left_me).wait_recv()
+    loads[2].wait()
+    offer[...] = meas[slot_other]
+    offer_copy = remote(offer, offered, send.at[0], recv.at[0], (partner, o))
+    start(offer_copy)
     left_mul(e_h)
-    meas_copy(1, 2 * left_me, 2, right_me).wait_recv()
-    start(meas_copy(3, 2 * left_me, 1, right_me))
-    start(meas_copy(4, 2 * left_me, 2, partner))
-    meas_copy(2, 2 * right_me, 2, left_me).wait_recv()
-    start(meas_copy(5, 2 * right_me + 1, 1, left_me))
-    start(meas_copy(6, 2 * right_me, 2, partner))
     right_mul(e_c, arr)
+    offer_copy.wait_recv()
+    chosen[...] = jnp.where(half_has == core, meas[slot_has], offered[...])
+    rise = remote(chosen, pattern, send.at[4], recv.at[4], (s, up))
+
+    @pl.when(core == 1)
+    def _():
+        rise.start()
+
     window(1)
 
     def second(rows, i):
@@ -239,20 +252,16 @@
             put(m, rows, i, pr * re - pi * im, pr * im + pi * re)
 
     by_rows(second)
-    meas_copy(3, 2 * far_me, 1, right_me).wait_recv()
-    start(meas_copy(7, 2 * far_me, 1, partner))
-    meas_copy(5, 2 * far_me + 1, 1, left_me).wait_recv()
-    start(meas_copy(8, 2 * far_me + 1, 1, partner))
     left_mul(e_f)
     right_mul(e_i, far)
-    loads[2].wait()
-    meas_copy(0, 2 * partner, 2, partner).wait_recv()
-    meas_copy(4, 2 * left_ot, 2, partner).wait_recv()
-    meas_copy(6, 2 * right_ot, 2, partner).wait_recv()
-    meas_copy(7, 2 * far_ot, 1, partner).wait_recv()
-    meas_copy(8, 2 * far_ot + 1, 1, partner).wait_recv()
-
-    pattern[...] = meas[source]
+
+    @pl.when(core == 0)
+    def _():
+        pattern[...] = chosen[...]
+
+    @pl.when(core == 1)
+    def _():
+        rise.wait_recv()
 
     def misfit(rows, i):
         parts = [(far[m, 0, rows, :], far[m, 1, rows, :]) for m in range(2)]
@@ -273,25 +282,25 @@
         return pl.ds(first, half) if part is None else pl.ds(first + part * half // 2, half // 2)
 
     def near(j, c, side):
-        layer, q = chunks[j][0], 11 + 14 * j + (2 if side else 4)
+        layer, q = chunks[j][0], 11 + 16 * j + (2 if side else 4)
         peer = (right if side else left)[c]
         return remote(
             gsend.at[layer, c, span(j)], wins.at[layer, s, span(j)], send.at[q + c], recv.at[q + core], (peer, o)
         )
 
     def near_in(j, c, side):
-        layer, q = chunks[j][0], 11 + 14 * j + (2 if side else 4)
+        layer, q = chunks[j][0], 11 + 16 * j + (2 if side else 4)
         slot = wins.at[layer, (left if side else right)[c], span(j)]
         return remote(slot, slot, send.at[q + c], recv.at[q + c], (partner, o))
 
     def relay(j, c, side, incoming=False):
-        q = 11 + 14 * j + (6 if side else 8) + c
+        q = 11 + 16 * j + (6 if side else 8) + c
         owner = far_at[c] if incoming else (left if side else right)[c]
         piece = wins.at[chunks[j][0], owner, span(j, 0 if side else 1)]
         return remote(piece, piece, send.at[q], recv.at[q], (right_me if side else left_me, o))
 
     def pair(j, incoming=False):
-        layer, q = chunks[j][0], 11 + 14 * j
+        layer, q = chunks[j][0], 11 + 16 * j
         slot = wins.at[layer, partner if incoming else s, span(j)]
         return remote(gsend.at[layer, other, span(j)], slot, send.at[q], recv.at[q], (partner, o))
 
@@ -320,7 +329,7 @@
     lane = lax.broadcasted_iota(jnp.int32, (1, N), 1)
     cols = [
         [jnp.where((lane + (2 * x + b) * N >= c0) & (lane + (2 * x + b) * N < c0 + N), 1.0, 0.0) for b in range(2)]
-        for _, _, c0 in places
+        for _, c0 in places
     ]
 
     def gather(j):
@@ -331,36 +340,42 @@
             at = pl.multiple_of(first + i * chunk, chunk)
             rows = pl.ds(at, chunk)
             line = lax.broadcasted_iota(jnp.int32, (chunk, N), 0) + at
-            sums = [[jnp.zeros((chunk, N), F32) for _ in range(2)] for _ in range(2)]
+            sums = [[jnp.zeros((chunk, N), F32) for _ in range(3)] for _ in range(2)]
             for n in range(NS):
                 term = wins[layer, n, rows, :].astype(F32)
-                above = line >= places[n][1]
+                above = line >= places[n][0]
                 for b in range(2):
                     masked = term * cols[n][b]
-                    sums[b][0] = sums[b][0] + jnp.where(above, masked, 0.0)
-                    sums[b][1] = sums[b][1] + jnp.where(above, 0.0, masked)
+                    low, high = (2, 0) if n % 2 else (0, 1)
+                    sums[b][low] = sums[b][low] + jnp.where(above, masked, 0.0)
+                    sums[b][high] = sums[b][high] + jnp.where(above, 0.0, masked)
             mine = core == 0
             acc[layer, rows, :] = jnp.where(mine, sums[0][0], sums[1][0])
             tsend[layer, rows, :] = jnp.where(mine, sums[1][0], sums[0][0]).astype(BF)
             for b in range(2):
                 bsend[layer, b, rows, :] = sums[b][1].astype(BF)
+                csend[layer, b, rows, :] = sums[b][2].astype(BF)
             return carry
 
         lax.fori_loop(0, half // chunk, run, 0)
 
     def top_copy(j):
-        layer, q = chunks[j][0], 21 + 14 * j
+        layer, q = chunks[j][0], 21 + 16 * j
         return remote(tsend.at[layer, span(j)], trecv.at[layer, span(j)], send.at[q], recv.at[q], (partner, o))
 
-    def bottom_copy(j, b):
-        layer, q = chunks[j][0], 22 + 14 * j
+    def edge(j, upward):
+        q = 22 + 16 * j + (0 if upward else 2)
+        return (bsend, brecv, q, up) if upward else (csend, crecv, q, down)
+
+    def edge_copy(j, b, upward):
+        layer, (source, target, q, to) = chunks[j][0], edge(j, upward)
         return remote(
-            bsend.at[layer, b, span(j)], brecv.at[layer, core, span(j)], send.at[q + b], recv.at[q + core], (2 * x + b, up)
+            source.at[layer, b, span(j)], target.at[layer, core, span(j)], send.at[q + b], recv.at[q + core], (2 * x + b, to)
         )
 
-    def bottom_in(j, c):
-        layer, q = chunks[j][0], 22 + 14 * j
-        return remote(bsend.at[layer, c, span(j)], brecv.at[layer, c, span(j)], send.at[q + c], recv.at[q + c], (s, up))
+    def edge_in(j, c, upward):
+        layer, (source, target, q, to) = chunks[j][0], edge(j, upward)
+        return remote(source.at[layer, c, span(j)], target.at[layer, c, span(j)], send.at[q + c], recv.at[q + c], (s, to))
 
     def collect(j):
         pair(j, True).wait_recv()
@@ -369,20 +384,21 @@
                 relay(j, c, side, True).wait_recv()
         gather(j)
         for b in range(2):
-            start(bottom_copy(j, b))
+            start(edge_copy(j, b, True))
+            start(edge_copy(j, b, False))
         start(top_copy(j))
 
     def finish(j):
         layer = chunks[j][0]
         top_copy(j).wait_recv()
         for c in range(2):
-            bottom_in(j, c).wait_recv()
+            edge_in(j, c, True).wait_recv()
+            edge_in(j, c, False).wait_recv()
         for i in range(2):
             rows = span(j, i)
-            done[layer, core, rows, :] = acc[layer, rows, :] + brecv[layer, core, rows, :].astype(F32)
-            done[layer, other, rows, :] = (
-                trecv[layer, rows, :].astype(F32) + brecv[layer, other, rows, :].astype(F32)
-            )
+            rims = [brecv[layer, c, rows, :].astype(F32) + crecv[layer, c, rows, :].astype(F32) for c in (core, other)]
+            done[layer, core, rows, :] = acc[layer, rows, :] + rims[0]
+            done[layer, other, rows, :] = trecv[layer, rows, :].astype(F32) + rims[1]
         leaving = pltpu.make_async_copy(
             done.at[layer, :, span(j)], out_hbm.at[layer, :, span(j)], dma.at[6 + 2 * NS + j]
         )
@@ -411,7 +427,7 @@
             esend[m, 1, rows, :] = (re * ci - im * cr).astype(BF)
 
     by_rows(leave)
-    q_pair, q_y, q_z, q_x = 67, 68, 71, 78
+    q_pair, q_y, q_z, q_x = 75, 76, 79, 86
     e_copy = remote(esend.at[other], erecv, send.at[q_pair], recv.at[q_pair], (partner, o))
     start(e_copy)
     share(0, probe, cur)
@@ -491,10 +507,22 @@
     for copy in sends:
         copy.wait_send()
 
-
-def hand_on(grad_ref, probe_ref, grad_out, probe_out):
-    grad_out[...] = grad_ref[...]
-    probe_out[...] = probe_ref[...]
+    @pl.when(core == 1)
+    def _():
+        rise.wait_send()
+
+
+def hand_on(grad_hbm, probe_hbm, grad_out, probe_out, held, probe_held, sem):
+    moves = [(grad_hbm.at[a], held.at[a], grad_out.at[a]) for a in range(4)] + [(probe_hbm, probe_held, probe_out)]
+    inward = [pltpu.make_async_copy(source, kept, sem.at[i]) for i, (source, kept, _) in enumerate(moves)]
+    outward = [pltpu.make_async_copy(kept, target, sem.at[5 + i]) for i, (_, kept, target) in enumerate(moves)]
+    for copy in inward:
+        copy.start()
+    for copy, after in zip(inward, outward):
+        copy.wait()
+        after.start()
+    for copy in outward:
+        copy.wait()
 
 
 def body(object_slices, probe, measured, positions, counts):
@@ -516,13 +544,13 @@
             pltpu.SMEM((2 * NS, 1, 128), jnp.int32),
             *[vmem(square(NS, 2), F32)] * 2,
             vmem(square(2, 2), F32),
-            vmem(square(16), BF),
+            vmem(square(2 * NX), BF),
             vmem(square(4), BF),
             *[vmem((2 * N, 2 * N), BF)] * 4,
             vmem(square(2, 2), BF),
             vmem(square(2, 2), BF),
             vmem(square(2, 2), BF),
-            vmem(square(), BF),
+            *[vmem(square(), BF)] * 4,
             vmem(square(2, 2), F32),
             vmem((2 * N, 2 * N), BF),
             vmem((2 * N, 2 * N), BF),
@@ -535,8 +563,7 @@
             vmem(square(2, 2), F32),
             vmem(square(2), BF),
             vmem(square(2), BF),
-            vmem(square(2, 2), BF),
-            vmem(square(2, 2), BF),
+            *[vmem(square(2, 2), BF)] * 4,
             vmem(square(2, 2), BF),
             vmem(square(2), BF),
             vmem(square(2), BF),
@@ -545,24 +572,23 @@
             vmem((NZ - 1, 16, N), BF),
             vmem((NS, 16, N), BF),
             pltpu.SemaphoreType.DMA((10 + 2 * NS,)),
-            pltpu.SemaphoreType.DMA((101,)),
-            pltpu.SemaphoreType.DMA((101,)),
+            pltpu.SemaphoreType.DMA((109,)),
+            pltpu.SemaphoreType.DMA((109,)),
         ],
         compiler_params=pltpu.CompilerParams(
             collective_id=0, has_side_effects=True, vmem_limit_bytes=60 * 1024 * 1024
         ),
         name="gradient",
     )(counts, positions[0, 0], object_slices, probe, measured[0, 0], tables())
-    plane = pl.BlockSpec((1, 1, N, N), lambda a, b: (a, b, 0, 0))
-    whole = pl.BlockSpec((2, 2, 8, 32), lambda a, b: (0, 0, 0, 0))
-    return pl.pallas_call(
+    grad, probe_grad = pl.pallas_call(
         hand_on,
-        out_shape=tuple(jax.ShapeDtypeStruct(r.shape, F32) for r in results),
-        grid=(2, 2),
-        in_specs=[plane, whole],
-        out_specs=(plane, whole),
+        out_shape=(jax.ShapeDtypeStruct(square(4), F32), jax.ShapeDtypeStruct((2, 2, 8, 32), F32)),
+        in_specs=[any_spec] * 2,
+        out_specs=(any_spec, any_spec),
+        scratch_shapes=[vmem(square(4), F32), vmem((2, 2, 8, 32), F32), pltpu.SemaphoreType.DMA((10,))],
         name="results",
-    )(*results)
+    )(results[0].reshape(square(4)), results[1])
+    return grad.reshape(square(2, 2)), probe_grad
 
 
 def solution(mesh):

time: 70.9 us -> 63.4 us (0.89)
  Pallas kernels: 69.5 us -> 62 us
    pallas_call x1, Pallas kernels: 66.1 us -> 60 us  [body(): pl.pallas_call(main_kernel, out_shape=(jax.ShapeDtypeStruct(square(2, 2),...]
    pallas_call x1, Pallas kernels: 3.38 us -> 2 us  [body(): pl.pallas_call(hand_on, out_shape=(jax.ShapeDtypeStruct(square(4), F32),...]
where the time goes in v5:
time: 63.4 us; the launch traced here: 63.3 us
  Pallas kernels  62 us (98%)
  between operations  1.29 us (2%)
    pallas_call x1, Pallas kernels, body(): pl.pallas_call(main_kernel, out_shape=(jax.ShapeDtypeStruct(square(2, 2),...  60 us
    pallas_call x1, Pallas kernels, body(): pl.pallas_call(hand_on, out_shape=(jax.ShapeDtypeStruct(square(4), F32),...  2 us

profile of v5, /device:TPU:1, one launch (start us, length us, event | category | flops | bytes accessed | tf_op | source)
XLA Modules:
  0.0 63.3 jit_solution(13693100929472998349)
XLA Ops:
  1.3 60.0 %gradient.1 = (f32[2,2,256,256]{3,2,1,0:T(8,128)}, f32[2,2,8,32]{3,2,1,0:T(8,128)}) custom-call(s32[1,1]{1,0:T(1,128)S(6)} %copy.8.count_ref, s32[2,2]{1,0:T(2,128)} %bitcast.6, f32[2,2,256,2048]{3,2,1,0:T(8,128)} %tile_hbm.1, f32[2,2,256,256]{3,2,1,0:T(8,128)} %probe_hbm.1, bf16[2,256,256]{2,1,0:T(8,128)(2,1)} %bitcast.5, ...), custom_call_target="tpu_custom_call" | custom-call | tf_op jit(solution)/shard_map/gradient/pallas_call | solution.py:532
  61.3 2.0 %results.1 = (f32[4,256,256]{2,1,0:T(8,128)}, f32[2,2,8,32]{3,2,1,0:T(8,128)}) custom-call(f32[4,256,256]{2,1,0:T(8,128)} %bitcast.4, f32[2,2,8,32]{3,2,1,0:T(8,128)} %get-tuple-element.7.probe_hbm), custom_call_target="tpu_custom_call" | custom-call | tf_op jit(solution)/shard_map/results/pallas_call | solution.py:583

commit v6 on v5

--- a/solution.py
+++ b/solution.py
@@ -40,7 +40,7 @@
 
 def main_kernel(
     count_ref, pos_hbm, tile_hbm, probe_hbm, meas_hbm, table_hbm, out_hbm, pout_ref,
-    pos_ref, row, rows_in, tab, tile_0, tile_1, probe, meas, tabs, e_f, e_i, e_h, e_c, hsend, hrecv, local, offer, offered, chosen, pattern, win, v, u, arr, far, cur,
+    pos_ref, row, rows_in, tab, tile_0, tile_1, probe, meas, tabs, e_f, e_i, e_h, e_c, hsend, hrecv, local, offer, offered, rising, risen, pattern, win, v, u, arr, far, cur,
     gsend, wins, acc, done, tsend, trecv, bsend, brecv, csend, crecv, esend, erecv, ysend, yrecv, zsend, zrecv, xall,
     dma, send, recv,
 ):
@@ -126,8 +126,8 @@
     every = [(k, base) for base in (0, NS) for k in range(NS) if base or k]
     for k, base in every:
         start(place_copy(k, base, s))
-    for q, peer in ((1, right_me), (2, left_me)):
-        start(remote(meas_hbm, meas.at[pl.ds(2 * x, 2)], send.at[q], recv.at[q], (peer, o)))
+    for q, k, peer in ((1, 0, right_me), (2, 1, left_me), (6, 1, right_me), (7, 0, left_me)):
+        start(remote(meas_hbm.at[pl.ds(k, 1)], meas.at[pl.ds(2 * x + k, 1)], send.at[q], recv.at[q], (peer, o)))
     loads[0].wait()
     for e_ref, re, im, sign in ((e_f, 0, 1, 1), (e_i, 0, 1, -1), (e_h, 2, 3, 1), (e_c, 2, 3, -1)):
         e_ref[0:N, 0:N] = tabs[re]
@@ -158,24 +158,29 @@
     pick_out = picks(col_out - k_out * N)
     halo_to = jnp.where(core == 0, down, up)
 
-    def halo_copy(layer):
-        return remote(hsend.at[layer], hrecv.at[layer], send.at[9 + layer], recv.at[9 + layer], (s, halo_to))
+    def halo_copy(layer, part):
+        q = 111 + 2 * layer + part
+        return remote(hsend.at[layer, part], hrecv.at[layer, part], send.at[q], recv.at[q], (s, halo_to))
 
     for layer in range(2):
         for b in range(NS):
             loads[3 + NS * layer + b].wait()
         for part in range(2):
             hsend[layer, part] = columns(layer, part, k_out, pick_out)
-        start(halo_copy(layer))
-    _, _, row0, col0 = assigned(NS * core, x + NX * core)
+            start(halo_copy(layer, part))
+    meas_copy(1, 2 * x_left, 1, right_me).wait_recv()
+    start(meas_copy(3, 2 * x_left, 1, right_me))
+    meas_copy(2, 2 * x_right + 1, 1, left_me).wait_recv()
+    start(meas_copy(5, 2 * x_right + 1, 1, left_me))
+    half_mine, slot_mine, row0, col0 = assigned(NS * core, x + NX * core)
     k_own = col_block(col0)
     pick_own = picks(col0 - k_own * N)
     for layer in range(2):
         for part in range(2):
             local[layer, part] = columns(layer, part, k_own, pick_own)
     places = [assigned(NS * (d % 2), d // 2 + NX * (d % 2))[2:] for d in range(NS)]
-    half_has, slot_has, _, _ = assigned(0, x + NX * core)
-    _, slot_other, _, _ = assigned(0, x + NX * other)
+    _, slot_a, _, _ = assigned(0, x)
+    _, slot_b, _, _ = assigned(0, x + NX)
     rows_own = one_hot((N, N), lambda a, b: b + N * core == a + row0)
     rows_halo = one_hot((N, N), lambda a, b: b + N * other == a + row0)
     turn = jnp.where(col0 == 7 * N, 0, col0 - k_own * N)
@@ -184,8 +189,8 @@
     loads[1].wait()
 
     def window(layer):
-        halo_copy(layer).wait_recv()
         for part in range(2):
+            halo_copy(layer, part).wait_recv()
             win[layer, part] = dot(rows_own, local[layer, part]) + dot(rows_halo, hrecv[layer, part])
 
     step = 32
@@ -213,11 +218,6 @@
             result[0, part] = product[0:N]
             result[1, part] = product[N:]
 
-    meas_copy(1, 2 * x_left, 2, right_me).wait_recv()
-    start(meas_copy(3, 2 * x_left, 1, right_me))
-    meas_copy(2, 2 * x_right, 2, left_me).wait_recv()
-    start(meas_copy(5, 2 * x_right + 1, 1, left_me))
-
     window(0)
 
     def enter(rows, i):
@@ -227,22 +227,20 @@
             put(m, rows, i, pr * re - pi * im, pr * im + pi * re)
 
     by_rows(enter)
-    meas_copy(3, 2 * x_far, 1, right_me).wait_recv()
-    meas_copy(5, 2 * x_far + 1, 1, left_me).wait_recv()
+    for q, slot, peer in ((3, 2 * x_far, right_me), (5, 2 * x_far + 1, left_me), (6, 2 * x_left + 1, right_me), (7, 2 * x_right, left_me)):
+        meas_copy(q, slot, 1, peer).wait_recv()
     loads[2].wait()
-    offer[...] = meas[slot_other]
-    offer_copy = remote(offer, offered, send.at[0], recv.at[0], (partner, o))
-    start(offer_copy)
+    rising[...] = meas[slot_b]
+    start(remote(rising, risen.at[core], send.at[109], recv.at[109 + core], (2 * x + 1, up)))
+    offer[...] = meas[slot_a]
+    offer_copy = remote(offer, offered, send.at[0], recv.at[0], (2 * x, o))
+
+    @pl.when(core == 1)
+    def _():
+        offer_copy.start()
+
     left_mul(e_h)
     right_mul(e_c, arr)
-    offer_copy.wait_recv()
-    chosen[...] = jnp.where(half_has == core, meas[slot_has], offered[...])
-    rise = remote(chosen, pattern, send.at[4], recv.at[4], (s, up))
-
-    @pl.when(core == 1)
-    def _():
-        rise.start()
-
     window(1)
 
     def second(rows, i):
@@ -257,11 +255,14 @@
 
     @pl.when(core == 0)
     def _():
-        pattern[...] = chosen[...]
+        offer_copy.wait_recv()
+        pattern[...] = jnp.where(half_mine == 0, offer[...], offered[...])
 
     @pl.when(core == 1)
     def _():
-        rise.wait_recv()
+        for c in range(2):
+            remote(rising, risen.at[c], send.at[109], recv.at[109 + c], (s, up)).wait_recv()
+        pattern[...] = jnp.where(half_mine == 0, risen[0], risen[1])
 
     def misfit(rows, i):
         parts = [(far[m, 0, rows, :], far[m, 1, rows, :]) for m in range(2)]
@@ -274,12 +275,11 @@
     left_mul(e_i)
     right_mul(e_f, cur)
 
-    half = N // 2
-    chunks = [(1, 0), (1, 1), (0, 0), (0, 1)]
+    chunks = [(1, 0, 128), (1, 128, 128), (0, 0, 160), (0, 160, 96)]
 
     def span(j, part=None):
-        first = chunks[j][1] * half
-        return pl.ds(first, half) if part is None else pl.ds(first + part * half // 2, half // 2)
+        _, first, size = chunks[j]
+        return pl.ds(first, size) if part is None else pl.ds(first + part * size // 2, size // 2)
 
     def near(j, c, side):
         layer, q = chunks[j][0], 11 + 16 * j + (2 if side else 4)
@@ -333,7 +333,7 @@
     ]
 
     def gather(j):
-        layer, first = chunks[j][0], chunks[j][1] * half
+        layer, first, size = chunks[j]
         chunk = 16
 
         def run(i, carry):
@@ -357,7 +357,7 @@
                 csend[layer, b, rows, :] = sums[b][2].astype(BF)
             return carry
 
-        lax.fori_loop(0, half // chunk, run, 0)
+        lax.fori_loop(0, size // chunk, run, 0)
 
     def top_copy(j):
         layer, q = chunks[j][0], 21 + 16 * j
@@ -451,7 +451,6 @@
     pass_on(0)
     launch(2)
     pass_on(1)
-    launch(3)
     for copy in y_copies:
         copy.wait_recv()
     rows_me = pl.ds(pl.multiple_of(y * deep, deep), deep)
@@ -473,6 +472,7 @@
         z_copies.append(copy)
     collect(0)
     pass_on(2)
+    launch(3)
     collect(1)
     for copy in z_copies:
         copy.wait_recv()
@@ -509,7 +509,7 @@
 
     @pl.when(core == 1)
     def _():
-        rise.wait_send()
+        offer_copy.wait_send()
 
 
 def hand_on(grad_hbm, probe_hbm, grad_out, probe_out, held, probe_held, sem):
@@ -550,7 +550,9 @@
             vmem(square(2, 2), BF),
             vmem(square(2, 2), BF),
             vmem(square(2, 2), BF),
-            *[vmem(square(), BF)] * 4,
+            *[vmem(square(), BF)] * 3,
+            vmem(square(2), BF),
+            vmem(square(), BF),
             vmem(square(2, 2), F32),
             vmem((2 * N, 2 * N), BF),
             vmem((2 * N, 2 * N), BF),
@@ -572,8 +574,8 @@
             vmem((NZ - 1, 16, N), BF),
             vmem((NS, 16, N), BF),
             pltpu.SemaphoreType.DMA((10 + 2 * NS,)),
-            pltpu.SemaphoreType.DMA((109,)),
-            pltpu.SemaphoreType.DMA((109,)),
+            pltpu.SemaphoreType.DMA((115,)),
+            pltpu.SemaphoreType.DMA((115,)),
         ],
         compiler_params=pltpu.CompilerParams(
             collective_id=0, has_side_effects=True, vmem_limit_bytes=60 * 1024 * 1024

time: 63.4 us -> 62.4 us (0.984)
  Pallas kernels: 62 us -> 61 us
    pallas_call x1, Pallas kernels: 60 us -> 59 us  [body(): pl.pallas_call(main_kernel, out_shape=(jax.ShapeDtypeStruct(square(2, 2),...]
where the time goes in v6:
time: 62.4 us; the launch traced here: 62.3 us
  Pallas kernels  61 us (98%)
  between operations  1.29 us (2%)
    pallas_call x1, Pallas kernels, body(): pl.pallas_call(main_kernel, out_shape=(jax.ShapeDtypeStruct(square(2, 2),...  59 us
    pallas_call x1, Pallas kernels, body(): pl.pallas_call(hand_on, out_shape=(jax.ShapeDtypeStruct(square(4), F32),...  2 us

profile of v6, /device:TPU:1, one launch (start us, length us, event | category | flops | bytes accessed | tf_op | source)
XLA Modules:
  0.0 62.3 jit_solution(1828845656783917585)
XLA Ops:
  1.3 59.0 %gradient.1 = (f32[2,2,256,256]{3,2,1,0:T(8,128)}, f32[2,2,8,32]{3,2,1,0:T(8,128)}) custom-call(s32[1,1]{1,0:T(1,128)S(6)} %copy.8.count_ref, s32[2,2]{1,0:T(2,128)} %bitcast.6, f32[2,2,256,2048]{3,2,1,0:T(8,128)} %tile_hbm.1, f32[2,2,256,256]{3,2,1,0:T(8,128)} %probe_hbm.1, bf16[2,256,256]{2,1,0:T(8,128)(2,1)} %bitcast.5, ...), custom_call_target="tpu_custom_call" | custom-call | tf_op jit(solution)/shard_map/gradient/pallas_call | solution.py:532
  60.3 2.0 %results.1 = (f32[4,256,256]{2,1,0:T(8,128)}, f32[2,2,8,32]{3,2,1,0:T(8,128)}) custom-call(f32[4,256,256]{2,1,0:T(8,128)} %bitcast.4, f32[2,2,8,32]{3,2,1,0:T(8,128)} %get-tuple-element.7.probe_hbm), custom_call_target="tpu_custom_call" | custom-call | tf_op jit(solution)/shard_map/results/pallas_call | solution.py:585

commit v7 on v6

--- a/solution.py
+++ b/solution.py
@@ -121,7 +121,7 @@
 
     def place_copy(k, base, owner):
         peer = (rem(s + k, NS), up if base else o)
-        return remote(row, rows_in.at[base + owner], send.at[93 + base + k], recv.at[93 + base + k], peer)
+        return remote(row, rows_in.at[base + owner], send.at[109 + base + k], recv.at[109 + base + k], peer)
 
     every = [(k, base) for base in (0, NS) for k in range(NS) if base or k]
     for k, base in every:
@@ -159,7 +159,7 @@
     halo_to = jnp.where(core == 0, down, up)
 
     def halo_copy(layer, part):
-        q = 111 + 2 * layer + part
+        q = 127 + 2 * layer + part
         return remote(hsend.at[layer, part], hrecv.at[layer, part], send.at[q], recv.at[q], (s, halo_to))
 
     for layer in range(2):
@@ -218,6 +218,18 @@
             result[0, part] = product[0:N]
             result[1, part] = product[N:]
 
+    for q, slot, peer in ((3, 2 * x_far, right_me), (5, 2 * x_far + 1, left_me), (6, 2 * x_left + 1, right_me), (7, 2 * x_right, left_me)):
+        meas_copy(q, slot, 1, peer).wait_recv()
+    loads[2].wait()
+    rising[...] = meas[slot_b]
+    start(remote(rising, risen.at[core], send.at[125], recv.at[125 + core], (2 * x + 1, up)))
+    offer[...] = meas[slot_a]
+    offer_copy = remote(offer, offered, send.at[0], recv.at[0], (2 * x, o))
+
+    @pl.when(core == 1)
+    def _():
+        offer_copy.start()
+
     window(0)
 
     def enter(rows, i):
@@ -227,18 +239,6 @@
             put(m, rows, i, pr * re - pi * im, pr * im + pi * re)
 
     by_rows(enter)
-    for q, slot, peer in ((3, 2 * x_far, right_me), (5, 2 * x_far + 1, left_me), (6, 2 * x_left + 1, right_me), (7, 2 * x_right, left_me)):
-        meas_copy(q, slot, 1, peer).wait_recv()
-    loads[2].wait()
-    rising[...] = meas[slot_b]
-    start(remote(rising, risen.at[core], send.at[109], recv.at[109 + core], (2 * x + 1, up)))
-    offer[...] = meas[slot_a]
-    offer_copy = remote(offer, offered, send.at[0], recv.at[0], (2 * x, o))
-
-    @pl.when(core == 1)
-    def _():
-        offer_copy.start()
-
     left_mul(e_h)
     right_mul(e_c, arr)
     window(1)
@@ -261,7 +261,7 @@
     @pl.when(core == 1)
     def _():
         for c in range(2):
-            remote(rising, risen.at[c], send.at[109], recv.at[109 + c], (s, up)).wait_recv()
+            remote(rising, risen.at[c], send.at[125], recv.at[125 + c], (s, up)).wait_recv()
         pattern[...] = jnp.where(half_mine == 0, risen[0], risen[1])
 
     def misfit(rows, i):
@@ -275,7 +275,7 @@
     left_mul(e_i)
     right_mul(e_f, cur)
 
-    chunks = [(1, 0, 128), (1, 128, 128), (0, 0, 160), (0, 160, 96)]
+    chunks = [(1, 0, 128), (1, 128, 128), (0, 0, 96), (0, 96, 96), (0, 192, 64)]
 
     def span(j, part=None):
         _, first, size = chunks[j]
@@ -427,7 +427,7 @@
             esend[m, 1, rows, :] = (re * ci - im * cr).astype(BF)
 
     by_rows(leave)
-    q_pair, q_y, q_z, q_x = 75, 76, 79, 86
+    q_pair, q_y, q_z, q_x = 91, 92, 95, 102
     e_copy = remote(esend.at[other], erecv, send.at[q_pair], recv.at[q_pair], (partner, o))
     start(e_copy)
     share(0, probe, cur)
@@ -451,6 +451,7 @@
     pass_on(0)
     launch(2)
     pass_on(1)
+    launch(3)
     for copy in y_copies:
         copy.wait_recv()
     rows_me = pl.ds(pl.multiple_of(y * deep, deep), deep)
@@ -472,8 +473,9 @@
         z_copies.append(copy)
     collect(0)
     pass_on(2)
-    launch(3)
+    launch(4)
     collect(1)
+    pass_on(3)
     for copy in z_copies:
         copy.wait_recv()
     total = zsend[z].astype(F32)
@@ -485,9 +487,11 @@
         copy = remote(xall.at[0], xall.at[k], send.at[q_x + k - 1], recv.at[q_x + k - 1], (rem(s + k, NS), o))
         start(copy)
         x_copies.append(copy)
-    pass_on(3)
+    collect(2)
+    pass_on(4)
     finish(0)
-    collect(2)
+    finish(1)
+    collect(3)
     for copy in x_copies:
         copy.wait_recv()
     pick = one_hot((N, 128), lambda a, b: a == b + 32 * s)
@@ -498,10 +502,10 @@
     for part in range(2):
         pout_ref[core, part] = mine[8 * part : 8 * part + 8, :32]
         pout_ref[other, part] = theirs[8 * part : 8 * part + 8, :32]
-    finish(1)
-    collect(3)
+    collect(4)
     finish(2)
     finish(3)
+    finish(4)
     for copy in gone:
         copy.wait()
     for copy in sends:
@@ -573,9 +577,9 @@
             vmem((NZ, 16, N), BF),
             vmem((NZ - 1, 16, N), BF),
             vmem((NS, 16, N), BF),
-            pltpu.SemaphoreType.DMA((10 + 2 * NS,)),
-            pltpu.SemaphoreType.DMA((115,)),
-            pltpu.SemaphoreType.DMA((115,)),
+            pltpu.SemaphoreType.DMA((11 + 2 * NS,)),
+            pltpu.SemaphoreType.DMA((131,)),
+            pltpu.SemaphoreType.DMA((131,)),
         ],
         compiler_params=pltpu.CompilerParams(
             collective_id=0, has_side_effects=True, vmem_limit_bytes=60 * 1024 * 1024

time: 62.4 us -> 61.9 us (level)
  no operation moved by 1% of the time
where the time goes in v7:
time: 61.9 us; the launch traced here: 61.8 us
  Pallas kernels  60.5 us (98%)
  between operations  1.29 us (2%)
    pallas_call x1, Pallas kernels, body(): pl.pallas_call(main_kernel, out_shape=(jax.ShapeDtypeStruct(square(2, 2),...  58.5 us
    pallas_call x1, Pallas kernels, body(): pl.pallas_call(hand_on, out_shape=(jax.ShapeDtypeStruct(square(4), F32),...  2 us

profile of v7, /device:TPU:1, one launch (start us, length us, event | category | flops | bytes accessed | tf_op | source)
XLA Modules:
  0.0 61.8 jit_solution(11672185035045694229)
XLA Ops:
  1.3 58.5 %gradient.1 = (f32[2,2,256,256]{3,2,1,0:T(8,128)}, f32[2,2,8,32]{3,2,1,0:T(8,128)}) custom-call(s32[1,1]{1,0:T(1,128)S(6)} %copy.8.count_ref, s32[2,2]{1,0:T(2,128)} %bitcast.6, f32[2,2,256,2048]{3,2,1,0:T(8,128)} %tile_hbm.1, f32[2,2,256,256]{3,2,1,0:T(8,128)} %probe_hbm.1, bf16[2,256,256]{2,1,0:T(8,128)(2,1)} %bitcast.5, ...), custom_call_target="tpu_custom_call" | custom-call | tf_op jit(solution)/shard_map/gradient/pallas_call | solution.py:536
  59.8 2.0 %results.1 = (f32[4,256,256]{2,1,0:T(8,128)}, f32[2,2,8,32]{3,2,1,0:T(8,128)}) custom-call(f32[4,256,256]{2,1,0:T(8,128)} %bitcast.4, f32[2,2,8,32]{3,2,1,0:T(8,128)} %get-tuple-element.7.probe_hbm), custom_call_target="tpu_custom_call" | custom-call | tf_op jit(solution)/shard_map/results/pallas_call | solution.py:589

commit v8 on v7

--- a/solution.py
+++ b/solution.py
@@ -59,10 +59,10 @@
     sends, gone = [], []
 
     barrier = pltpu.get_barrier_semaphore()
-    peers = [(rem(s + k, NS), o) for k in range(1, NS)]
-    peers += [(s, up), (partner, up)] + [(rem(s + k, NS), down) for k in range(NS)]
-    peers += [(s, rem(y + k, NY) * NZ + z) for k in range(1, NY)]
-    peers += [(s, y * NZ + rem(z + k, NZ)) for k in range(1, NZ)]
+    peers = [(s, y * NZ + rem(z + k, NZ)) for k in (4, 3, 5, 2, 6, 1, 7)]
+    peers += [(rem(s + k, NS), down) for k in (4, 5, 3, 2, 6, 1, 7, 0)] + [(s, up), (partner, up)]
+    peers += [(rem(s + k, NS), o) for k in (4, 5, 3, 2, 6, 1, 7)]
+    peers += [(s, rem(y + k, NY) * NZ + z) for k in (2, 1, 3)]
     for peer in peers:
         pl.semaphore_signal(barrier, inc=1, device_id=peer, device_id_type=MESH)
 
@@ -275,7 +275,7 @@
     left_mul(e_i)
     right_mul(e_f, cur)
 
-    chunks = [(1, 0, 128), (1, 128, 128), (0, 0, 96), (0, 96, 96), (0, 192, 64)]
+    chunks = [(1, 0, 128), (1, 128, 128), (0, 0, 128), (0, 128, 64), (0, 192, 64)]
 
     def span(j, part=None):
         _, first, size = chunks[j]
@@ -304,7 +304,7 @@
         slot = wins.at[layer, partner if incoming else s, span(j)]
         return remote(gsend.at[layer, other, span(j)], slot, send.at[q], recv.at[q], (partner, o))
 
-    def share(layer, first, adjoint):
+    def share(layer, first, adjoint, ready=None):
         for part in range(2):
             if part == 0:
                 term = lambda m: first[m, 0] * adjoint[m, 0] + first[m, 1] * adjoint[m, 1]
@@ -312,6 +312,9 @@
                 term = lambda m: first[m, 0] * adjoint[m, 1] - first[m, 1] * adjoint[m, 0]
             grad = (term(0) + term(1)).astype(BF)
             gsend[layer, part] = dot(dot(turn_rows, grad).astype(BF), turn_cols).astype(BF)
+            if ready is not None:
+                start(near(ready, part, 1))
+                start(near(ready, part, 0))
         wins[layer, s] = gsend[layer, core]
 
     def launch(j):
@@ -405,8 +408,8 @@
         leaving.start()
         gone.append(leaving)
 
-    share(1, arr, cur)
-    launch(0)
+    share(1, arr, cur, ready=0)
+    start(pair(0))
     launch(1)
 
     def behind(rows, i):
@@ -489,9 +492,8 @@
         x_copies.append(copy)
     collect(2)
     pass_on(4)
-    finish(0)
-    finish(1)
     collect(3)
+    collect(4)
     for copy in x_copies:
         copy.wait_recv()
     pick = one_hot((N, 128), lambda a, b: a == b + 32 * s)
@@ -502,10 +504,8 @@
     for part in range(2):
         pout_ref[core, part] = mine[8 * part : 8 * part + 8, :32]
         pout_ref[other, part] = theirs[8 * part : 8 * part + 8, :32]
-    collect(4)
-    finish(2)
-    finish(3)
-    finish(4)
+    for j in range(len(chunks)):
+        finish(j)
     for copy in gone:
         copy.wait()
     for copy in sends:
@@ -516,16 +516,14 @@
         offer_copy.wait_send()
 
 
-def hand_on(grad_hbm, probe_hbm, grad_out, probe_out, held, probe_held, sem):
-    moves = [(grad_hbm.at[a], held.at[a], grad_out.at[a]) for a in range(4)] + [(probe_hbm, probe_held, probe_out)]
-    inward = [pltpu.make_async_copy(source, kept, sem.at[i]) for i, (source, kept, _) in enumerate(moves)]
-    outward = [pltpu.make_async_copy(kept, target, sem.at[5 + i]) for i, (_, kept, target) in enumerate(moves)]
-    for copy in inward:
+def hand_on(grad_ref, probe_ref, grad_out, probe_out, sem):
+    copies = [
+        pltpu.make_async_copy(grad_ref, grad_out, sem.at[0]),
+        pltpu.make_async_copy(probe_ref, probe_out, sem.at[1]),
+    ]
+    for copy in copies:
         copy.start()
-    for copy, after in zip(inward, outward):
-        copy.wait()
-        after.start()
-    for copy in outward:
+    for copy in copies:
         copy.wait()
 
 
@@ -533,6 +531,10 @@
     vmem = pltpu.VMEM
     square = lambda *lead: (*lead, N, N)
     any_spec = pl.BlockSpec(memory_space=pl.ANY)
+    given = [
+        pltpu.with_memory_space_constraint(value, pltpu.HBM)
+        for value in (positions[0, 0], object_slices, probe, measured[0, 0], jnp.asarray(tables()))
+    ]
     results = pl.pallas_call(
         main_kernel,
         out_shape=(
@@ -582,19 +584,19 @@
             pltpu.SemaphoreType.DMA((131,)),
         ],
         compiler_params=pltpu.CompilerParams(
-            collective_id=0, has_side_effects=True, vmem_limit_bytes=60 * 1024 * 1024
+            collective_id=0, has_side_effects=True, vmem_limit_bytes=44 * 1024 * 1024
         ),
         name="gradient",
-    )(counts, positions[0, 0], object_slices, probe, measured[0, 0], tables())
-    grad, probe_grad = pl.pallas_call(
+    )(counts, *given)
+    return pl.pallas_call(
         hand_on,
-        out_shape=(jax.ShapeDtypeStruct(square(4), F32), jax.ShapeDtypeStruct((2, 2, 8, 32), F32)),
+        out_shape=tuple(jax.ShapeDtypeStruct(r.shape, F32) for r in results),
         in_specs=[any_spec] * 2,
         out_specs=(any_spec, any_spec),
-        scratch_shapes=[vmem(square(4), F32), vmem((2, 2, 8, 32), F32), pltpu.SemaphoreType.DMA((10,))],
+        scratch_shapes=[pltpu.SemaphoreType.DMA((2,))],
+        compiler_params=pltpu.CompilerParams(vmem_limit_bytes=8 * 1024 * 1024),
         name="results",
-    )(results[0].reshape(square(4)), results[1])
-    return grad.reshape(square(2, 2)), probe_grad
+    )(*results)
 
 
 def solution(mesh):

time: 61.9 us -> 59.1 us (0.955)
  Pallas kernels: 60.5 us -> 57.7 us
    pallas_call x1, Pallas kernels: 58.5 us -> 56.7 us  [body(): pl.pallas_call(main_kernel, out_shape=(jax.ShapeDtypeStruct(square(2, 2),...]
    pallas_call x1, Pallas kernels: 2 us -> 0.99 us  [body(): pl.pallas_call(hand_on, out_shape=tuple((jax.ShapeDtypeStruct(r.shape, F3...]
where the time goes in v8:
time: 59.1 us; the launch traced here: 59 us
  Pallas kernels  57.7 us (98%)
  between operations  1.29 us (2%)
    pallas_call x1, Pallas kernels, body(): pl.pallas_call(main_kernel, out_shape=(jax.ShapeDtypeStruct(square(2, 2),...  56.7 us

profile of v8, /device:TPU:1, one launch (start us, length us, event | category | flops | bytes accessed | tf_op | source)
XLA Modules:
  0.0 59.0 jit_solution(17874371461981728297)
XLA Ops:
  1.3 56.7 %gradient.1 = (f32[2,2,256,256]{3,2,1,0:T(8,128)S(1)}, f32[2,2,8,32]{3,2,1,0:T(8,128)S(1)}) custom-call(s32[1,1]{1,0:T(1,128)S(6)} %copy.8.count_ref, s32[2,2]{1,0:T(2,128)} %bitcast.3, f32[2,2,256,2048]{3,2,1,0:T(8,128)} %tile_hbm.1, f32[2,2,256,256]{3,2,1,0:T(8,128)} %probe_hbm.1, bf16[2,256,256]{2,1,0:T(8,128)(2,1)} %bitcast.2, ...), custom_call_target="tpu_custom_call" | custom-call | tf_op jit(solution)/shard_map/gradient/pallas_call | solution.py:538
  58.0 1.0 %results.1 = (f32[2,2,256,256]{3,2,1,0:T(8,128)}, f32[2,2,8,32]{3,2,1,0:T(8,128)}) custom-call(f32[2,2,256,256]{3,2,1,0:T(8,128)S(1)} %get-tuple-element.4.grad_ref, f32[2,2,8,32]{3,2,1,0:T(8,128)S(1)} %get-tuple-element.5.probe_ref), custom_call_target="tpu_custom_call" | custom-call | tf_op jit(solution)/shard_map/results/pallas_call | solution.py:591

commit v9 on v8

--- a/solution.py
+++ b/solution.py
@@ -121,7 +121,7 @@
 
     def place_copy(k, base, owner):
         peer = (rem(s + k, NS), up if base else o)
-        return remote(row, rows_in.at[base + owner], send.at[109 + base + k], recv.at[109 + base + k], peer)
+        return remote(row, rows_in.at[base + owner], send.at[125 + base + k], recv.at[125 + base + k], peer)
 
     every = [(k, base) for base in (0, NS) for k in range(NS) if base or k]
     for k, base in every:
@@ -159,7 +159,7 @@
     halo_to = jnp.where(core == 0, down, up)
 
     def halo_copy(layer, part):
-        q = 127 + 2 * layer + part
+        q = 143 + 2 * layer + part
         return remote(hsend.at[layer, part], hrecv.at[layer, part], send.at[q], recv.at[q], (s, halo_to))
 
     for layer in range(2):
@@ -222,7 +222,7 @@
         meas_copy(q, slot, 1, peer).wait_recv()
     loads[2].wait()
     rising[...] = meas[slot_b]
-    start(remote(rising, risen.at[core], send.at[125], recv.at[125 + core], (2 * x + 1, up)))
+    start(remote(rising, risen.at[core], send.at[141], recv.at[141 + core], (2 * x + 1, up)))
     offer[...] = meas[slot_a]
     offer_copy = remote(offer, offered, send.at[0], recv.at[0], (2 * x, o))
 
@@ -261,7 +261,7 @@
     @pl.when(core == 1)
     def _():
         for c in range(2):
-            remote(rising, risen.at[c], send.at[125], recv.at[125 + c], (s, up)).wait_recv()
+            remote(rising, risen.at[c], send.at[141], recv.at[141 + c], (s, up)).wait_recv()
         pattern[...] = jnp.where(half_mine == 0, risen[0], risen[1])
 
     def misfit(rows, i):
@@ -275,7 +275,7 @@
     left_mul(e_i)
     right_mul(e_f, cur)
 
-    chunks = [(1, 0, 128), (1, 128, 128), (0, 0, 128), (0, 128, 64), (0, 192, 64)]
+    chunks = [(1, 0, 128), (1, 128, 128), (0, 0, 96), (0, 96, 96), (0, 192, 32), (0, 224, 32)]
 
     def span(j, part=None):
         _, first, size = chunks[j]
@@ -430,7 +430,7 @@
             esend[m, 1, rows, :] = (re * ci - im * cr).astype(BF)
 
     by_rows(leave)
-    q_pair, q_y, q_z, q_x = 91, 92, 95, 102
+    q_pair, q_y, q_z, q_x = 107, 108, 111, 118
     e_copy = remote(esend.at[other], erecv, send.at[q_pair], recv.at[q_pair], (partner, o))
     start(e_copy)
     share(0, probe, cur)
@@ -479,6 +479,7 @@
     launch(4)
     collect(1)
     pass_on(3)
+    launch(5)
     for copy in z_copies:
         copy.wait_recv()
     total = zsend[z].astype(F32)
@@ -493,7 +494,9 @@
     collect(2)
     pass_on(4)
     collect(3)
+    pass_on(5)
     collect(4)
+    collect(5)
     for copy in x_copies:
         copy.wait_recv()
     pick = one_hot((N, 128), lambda a, b: a == b + 32 * s)
@@ -579,9 +582,9 @@
             vmem((NZ, 16, N), BF),
             vmem((NZ - 1, 16, N), BF),
             vmem((NS, 16, N), BF),
-            pltpu.SemaphoreType.DMA((11 + 2 * NS,)),
-            pltpu.SemaphoreType.DMA((131,)),
-            pltpu.SemaphoreType.DMA((131,)),
+            pltpu.SemaphoreType.DMA((12 + 2 * NS,)),
+            pltpu.SemaphoreType.DMA((147,)),
+            pltpu.SemaphoreType.DMA((147,)),
         ],
         compiler_params=pltpu.CompilerParams(
             collective_id=0, has_side_effects=True, vmem_limit_bytes=44 * 1024 * 1024

time: 59.1 us -> 59.7 us (1.010)
  Pallas kernels: 57.7 us -> 58.4 us
    pallas_call x1, Pallas kernels: 56.7 us -> 57.4 us  [body(): pl.pallas_call(main_kernel, out_shape=(jax.ShapeDtypeStruct(square(2, 2),...]
where the time goes in v9:
time: 59.7 us
  Pallas kernels  58.4 us (98%)
  between operations  1.29 us (2%)
    pallas_call x1, Pallas kernels, body(): pl.pallas_call(main_kernel, out_shape=(jax.ShapeDtypeStruct(square(2, 2),...  57.4 us

profile of v9, /device:TPU:1, one launch (start us, length us, event | category | flops | bytes accessed | tf_op | source)
XLA Modules:
  0.0 59.7 jit_solution(13234763621735906370)
XLA Ops:
  1.3 57.4 %gradient.1 = (f32[2,2,256,256]{3,2,1,0:T(8,128)S(1)}, f32[2,2,8,32]{3,2,1,0:T(8,128)S(1)}) custom-call(s32[1,1]{1,0:T(1,128)S(6)} %copy.8.count_ref, s32[2,2]{1,0:T(2,128)} %bitcast.3, f32[2,2,256,2048]{3,2,1,0:T(8,128)} %tile_hbm.1, f32[2,2,256,256]{3,2,1,0:T(8,128)} %probe_hbm.1, bf16[2,256,256]{2,1,0:T(8,128)(2,1)} %bitcast.2, ...), custom_call_target="tpu_custom_call" | custom-call | tf_op jit(solution)/shard_map/gradient/pallas_call | solution.py:541
  58.7 1.0 %results.1 = (f32[2,2,256,256]{3,2,1,0:T(8,128)}, f32[2,2,8,32]{3,2,1,0:T(8,128)}) custom-call(f32[2,2,256,256]{3,2,1,0:T(8,128)S(1)} %get-tuple-element.4.grad_ref, f32[2,2,8,32]{3,2,1,0:T(8,128)S(1)} %get-tuple-element.5.probe_ref), custom_call_target="tpu_custom_call" | custom-call | tf_op jit(solution)/shard_map/results/pallas_call | solution.py:594

commit v10 on v8

--- a/solution.py
+++ b/solution.py
@@ -56,7 +56,12 @@
     far_at = [2 * rem(x + 2, NX) + c for c in range(2)]
     up, down = rem(o + 1, NO), rem(o + NO - 1, NO)
     tile = (tile_0, tile_1)
-    sends, gone = [], []
+    sends, gone, made = {}, [], []
+
+    def remote_at(src, dst, place, recv_sem, device):
+        copy = remote(src, dst, send.at[place], recv_sem, device)
+        made.append((copy, place))
+        return copy
 
     barrier = pltpu.get_barrier_semaphore()
     peers = [(s, y * NZ + rem(z + k, NZ)) for k in (4, 3, 5, 2, 6, 1, 7)]
@@ -112,22 +117,25 @@
     pl.semaphore_wait(barrier, len(peers))
 
     def start(copy):
+        place = next(i for c, i in made if c is copy)
+        if place in sends:
+            sends[place].wait_send()
         copy.start()
-        sends.append(copy)
+        sends[place] = copy
 
     def meas_copy(q, slot, n, peer):
         ref = meas.at[pl.ds(slot, n)]
-        return remote(ref, ref, send.at[q], recv.at[q], (peer, o))
+        return remote_at(ref, ref, q, recv.at[q], (peer, o))
 
     def place_copy(k, base, owner):
         peer = (rem(s + k, NS), up if base else o)
-        return remote(row, rows_in.at[base + owner], send.at[109 + base + k], recv.at[109 + base + k], peer)
+        return remote_at(row, rows_in.at[base + owner], 35 + base + k, recv.at[95 + base + k], peer)
 
     every = [(k, base) for base in (0, NS) for k in range(NS) if base or k]
     for k, base in every:
         start(place_copy(k, base, s))
     for q, k, peer in ((1, 0, right_me), (2, 1, left_me), (6, 1, right_me), (7, 0, left_me)):
-        start(remote(meas_hbm.at[pl.ds(k, 1)], meas.at[pl.ds(2 * x + k, 1)], send.at[q], recv.at[q], (peer, o)))
+        start(remote_at(meas_hbm.at[pl.ds(k, 1)], meas.at[pl.ds(2 * x + k, 1)], q, recv.at[q], (peer, o)))
     loads[0].wait()
     for e_ref, re, im, sign in ((e_f, 0, 1, 1), (e_i, 0, 1, -1), (e_h, 2, 3, 1), (e_c, 2, 3, -1)):
         e_ref[0:N, 0:N] = tabs[re]
@@ -159,8 +167,8 @@
     halo_to = jnp.where(core == 0, down, up)
 
     def halo_copy(layer, part):
-        q = 127 + 2 * layer + part
-        return remote(hsend.at[layer, part], hrecv.at[layer, part], send.at[q], recv.at[q], (s, halo_to))
+        q = 2 * layer + part
+        return remote_at(hsend.at[layer, part], hrecv.at[layer, part], 51 + q, recv.at[113 + q], (s, halo_to))
 
     for layer in range(2):
         for b in range(NS):
@@ -222,9 +230,9 @@
         meas_copy(q, slot, 1, peer).wait_recv()
     loads[2].wait()
     rising[...] = meas[slot_b]
-    start(remote(rising, risen.at[core], send.at[125], recv.at[125 + core], (2 * x + 1, up)))
+    start(remote_at(rising, risen.at[core], 55, recv.at[111 + core], (2 * x + 1, up)))
     offer[...] = meas[slot_a]
-    offer_copy = remote(offer, offered, send.at[0], recv.at[0], (2 * x, o))
+    offer_copy = remote_at(offer, offered, 0, recv.at[0], (2 * x, o))
 
     @pl.when(core == 1)
     def _():
@@ -261,7 +269,7 @@
     @pl.when(core == 1)
     def _():
         for c in range(2):
-            remote(rising, risen.at[c], send.at[125], recv.at[125 + c], (s, up)).wait_recv()
+            remote_at(rising, risen.at[c], 55, recv.at[111 + c], (s, up)).wait_recv()
         pattern[...] = jnp.where(half_mine == 0, risen[0], risen[1])
 
     def misfit(rows, i):
@@ -282,27 +290,27 @@
         return pl.ds(first, size) if part is None else pl.ds(first + part * size // 2, size // 2)
 
     def near(j, c, side):
-        layer, q = chunks[j][0], 11 + 16 * j + (2 if side else 4)
+        layer, q, sq = chunks[j][0], 8 + 14 * j + (1 if side else 3), 8 + 14 * (j % 2) + (1 if side else 3)
         peer = (right if side else left)[c]
-        return remote(
-            gsend.at[layer, c, span(j)], wins.at[layer, s, span(j)], send.at[q + c], recv.at[q + core], (peer, o)
+        return remote_at(
+            gsend.at[layer, c, span(j)], wins.at[layer, s, span(j)], sq + c, recv.at[q + core], (peer, o)
         )
 
     def near_in(j, c, side):
-        layer, q = chunks[j][0], 11 + 16 * j + (2 if side else 4)
+        layer, q, sq = chunks[j][0], 8 + 14 * j + (1 if side else 3), 8 + 14 * (j % 2) + (1 if side else 3)
         slot = wins.at[layer, (left if side else right)[c], span(j)]
-        return remote(slot, slot, send.at[q + c], recv.at[q + c], (partner, o))
+        return remote_at(slot, slot, sq + c, recv.at[q + c], (partner, o))
 
     def relay(j, c, side, incoming=False):
-        q = 11 + 16 * j + (6 if side else 8) + c
+        q, sq = 8 + 14 * j + (5 if side else 7) + c, 8 + 14 * (j % 2) + (5 if side else 7) + c
         owner = far_at[c] if incoming else (left if side else right)[c]
         piece = wins.at[chunks[j][0], owner, span(j, 0 if side else 1)]
-        return remote(piece, piece, send.at[q], recv.at[q], (right_me if side else left_me, o))
+        return remote_at(piece, piece, sq, recv.at[q], (right_me if side else left_me, o))
 
     def pair(j, incoming=False):
-        layer, q = chunks[j][0], 11 + 16 * j
+        layer, q, sq = chunks[j][0], 8 + 14 * j, 8 + 14 * (j % 2)
         slot = wins.at[layer, partner if incoming else s, span(j)]
-        return remote(gsend.at[layer, other, span(j)], slot, send.at[q], recv.at[q], (partner, o))
+        return remote_at(gsend.at[layer, other, span(j)], slot, sq, recv.at[q], (partner, o))
 
     def share(layer, first, adjoint, ready=None):
         for part in range(2):
@@ -363,22 +371,23 @@
         lax.fori_loop(0, size // chunk, run, 0)
 
     def top_copy(j):
-        layer, q = chunks[j][0], 21 + 16 * j
-        return remote(tsend.at[layer, span(j)], trecv.at[layer, span(j)], send.at[q], recv.at[q], (partner, o))
+        layer, q, sq = chunks[j][0], 17 + 14 * j, 17 + 14 * (j % 2)
+        return remote_at(tsend.at[layer, span(j)], trecv.at[layer, span(j)], sq, recv.at[q], (partner, o))
 
     def edge(j, upward):
-        q = 22 + 16 * j + (0 if upward else 2)
-        return (bsend, brecv, q, up) if upward else (csend, crecv, q, down)
+        more = 18 + (0 if upward else 2)
+        q, sq = more + 14 * j, more + 14 * (j % 2)
+        return (bsend, brecv, q, sq, up) if upward else (csend, crecv, q, sq, down)
 
     def edge_copy(j, b, upward):
-        layer, (source, target, q, to) = chunks[j][0], edge(j, upward)
-        return remote(
-            source.at[layer, b, span(j)], target.at[layer, core, span(j)], send.at[q + b], recv.at[q + core], (2 * x + b, to)
+        layer, (source, target, q, sq, to) = chunks[j][0], edge(j, upward)
+        return remote_at(
+            source.at[layer, b, span(j)], target.at[layer, core, span(j)], sq + b, recv.at[q + core], (2 * x + b, to)
         )
 
     def edge_in(j, c, upward):
-        layer, (source, target, q, to) = chunks[j][0], edge(j, upward)
-        return remote(source.at[layer, c, span(j)], target.at[layer, c, span(j)], send.at[q + c], recv.at[q + c], (s, to))
+        layer, (source, target, q, sq, to) = chunks[j][0], edge(j, upward)
+        return remote_at(source.at[layer, c, span(j)], target.at[layer, c, span(j)], sq + c, recv.at[q + c], (s, to))
 
     def collect(j):
         pair(j, True).wait_recv()
@@ -430,8 +439,8 @@
             esend[m, 1, rows, :] = (re * ci - im * cr).astype(BF)
 
     by_rows(leave)
-    q_pair, q_y, q_z, q_x = 91, 92, 95, 102
-    e_copy = remote(esend.at[other], erecv, send.at[q_pair], recv.at[q_pair], (partner, o))
+    q_pair, q_y, q_z, q_x = 78, 79, 82, 89
+    e_copy = remote_at(esend.at[other], erecv, q_pair - 42, recv.at[q_pair], (partner, o))
     start(e_copy)
     share(0, probe, cur)
     e_copy.wait_recv()
@@ -446,8 +455,8 @@
     for k in range(1, NY):
         y_to = rem(y + k, NY)
         rows_to = pl.ds(pl.multiple_of(y_to * deep, deep), deep)
-        copy = remote(
-            ysend.at[:, rows_to, :], yrecv.at[k - 1], send.at[q_y + k - 1], recv.at[q_y + k - 1], (s, y_to * NZ + z)
+        copy = remote_at(
+            ysend.at[:, rows_to, :], yrecv.at[k - 1], q_y + k - 43, recv.at[q_y + k - 1], (s, y_to * NZ + z)
         )
         start(copy)
         y_copies.append(copy)
@@ -469,8 +478,8 @@
     z_copies = []
     for k in range(1, NZ):
         z_to = rem(z + k, NZ)
-        copy = remote(
-            zsend.at[z_to], zrecv.at[k - 1], send.at[q_z + k - 1], recv.at[q_z + k - 1], (s, y * NZ + z_to)
+        copy = remote_at(
+            zsend.at[z_to], zrecv.at[k - 1], q_z + k - 43, recv.at[q_z + k - 1], (s, y * NZ + z_to)
         )
         start(copy)
         z_copies.append(copy)
@@ -487,7 +496,7 @@
     xall[0] = total.astype(BF)
     x_copies = []
     for k in range(1, NS):
-        copy = remote(xall.at[0], xall.at[k], send.at[q_x + k - 1], recv.at[q_x + k - 1], (rem(s + k, NS), o))
+        copy = remote_at(xall.at[0], xall.at[k], q_x + k - 43, recv.at[q_x + k - 1], (rem(s + k, NS), o))
         start(copy)
         x_copies.append(copy)
     collect(2)
@@ -508,7 +517,7 @@
         finish(j)
     for copy in gone:
         copy.wait()
-    for copy in sends:
+    for copy in sends.values():
         copy.wait_send()
 
     @pl.when(core == 1)
@@ -580,8 +589,8 @@
             vmem((NZ - 1, 16, N), BF),
             vmem((NS, 16, N), BF),
             pltpu.SemaphoreType.DMA((11 + 2 * NS,)),
-            pltpu.SemaphoreType.DMA((131,)),
-            pltpu.SemaphoreType.DMA((131,)),
+            pltpu.SemaphoreType.DMA((56,)),
+            pltpu.SemaphoreType.DMA((117,)),
         ],
         compiler_params=pltpu.CompilerParams(
             collective_id=0, has_side_effects=True, vmem_limit_bytes=44 * 1024 * 1024

time: 59.1 us -> 58.2 us (0.985)
  Pallas kernels: 57.7 us -> 56.8 us
    pallas_call x1, Pallas kernels: 56.7 us -> 55.8 us  [body(): pl.pallas_call(main_kernel, out_shape=(jax.ShapeDtypeStruct(square(2, 2),...]
where the time goes in v10:
time: 58.2 us; the launch traced here: 58.1 us
  Pallas kernels  56.8 us (98%)
  between operations  1.29 us (2%)
    pallas_call x1, Pallas kernels, body(): pl.pallas_call(main_kernel, out_shape=(jax.ShapeDtypeStruct(square(2, 2),...  55.8 us

profile of v10, /device:TPU:1, one launch (start us, length us, event | category | flops | bytes accessed | tf_op | source)
XLA Modules:
  0.0 58.1 jit_solution(5476456763015960039)
XLA Ops:
  1.3 55.8 %gradient.1 = (f32[2,2,256,256]{3,2,1,0:T(8,128)S(1)}, f32[2,2,8,32]{3,2,1,0:T(8,128)S(1)}) custom-call(s32[1,1]{1,0:T(1,128)S(6)} %copy.8.count_ref, s32[2,2]{1,0:T(2,128)} %bitcast.3, f32[2,2,256,2048]{3,2,1,0:T(8,128)} %tile_hbm.1, f32[2,2,256,256]{3,2,1,0:T(8,128)} %probe_hbm.1, bf16[2,256,256]{2,1,0:T(8,128)(2,1)} %bitcast.2, ...), custom_call_target="tpu_custom_call" | custom-call | tf_op jit(solution)/shard_map/gradient/pallas_call | solution.py:547
  57.1 1.0 %results.1 = (f32[2,2,256,256]{3,2,1,0:T(8,128)}, f32[2,2,8,32]{3,2,1,0:T(8,128)}) custom-call(f32[2,2,256,256]{3,2,1,0:T(8,128)S(1)} %get-tuple-element.4.grad_ref, f32[2,2,8,32]{3,2,1,0:T(8,128)S(1)} %get-tuple-element.5.probe_ref), custom_call_target="tpu_custom_call" | custom-call | tf_op jit(solution)/shard_map/results/pallas_call | solution.py:600

commit v11 on v10

--- a/solution.py
+++ b/solution.py
@@ -129,7 +129,7 @@
 
     def place_copy(k, base, owner):
         peer = (rem(s + k, NS), up if base else o)
-        return remote_at(row, rows_in.at[base + owner], 35 + base + k, recv.at[95 + base + k], peer)
+        return remote_at(row, rows_in.at[base + owner], 35 + base + k, recv.at[82 + base // NS], peer)
 
     every = [(k, base) for base in (0, NS) for k in range(NS) if base or k]
     for k, base in every:
@@ -143,8 +143,11 @@
         e_ref[0:N, N:] = -tabs[im] if sign > 0 else tabs[im]
         e_ref[N:, 0:N] = tabs[im] if sign > 0 else -tabs[im]
 
-    for k, base in every:
-        place_copy(k, base, rem(s + NS - k, NS)).wait_recv()
+    def await_all(ref, place):
+        remote_at(ref, ref, 0, recv.at[place], (partner, o)).wait_recv()
+
+    await_all(rows_in.at[pl.ds(0, NS - 1)], 82)
+    await_all(rows_in.at[pl.ds(NS, NS)], 83)
     fetch = pltpu.make_async_copy(rows_in, tab, dma.at[3 + 2 * NS])
     fetch.start()
     fetch.wait()
@@ -168,7 +171,7 @@
 
     def halo_copy(layer, part):
         q = 2 * layer + part
-        return remote_at(hsend.at[layer, part], hrecv.at[layer, part], 51 + q, recv.at[113 + q], (s, halo_to))
+        return remote_at(hsend.at[layer, part], hrecv.at[layer, part], 51 + q, recv.at[86 + q], (s, halo_to))
 
     for layer in range(2):
         for b in range(NS):
@@ -230,7 +233,7 @@
         meas_copy(q, slot, 1, peer).wait_recv()
     loads[2].wait()
     rising[...] = meas[slot_b]
-    start(remote_at(rising, risen.at[core], 55, recv.at[111 + core], (2 * x + 1, up)))
+    start(remote_at(rising, risen.at[core], 55, recv.at[84 + core], (2 * x + 1, up)))
     offer[...] = meas[slot_a]
     offer_copy = remote_at(offer, offered, 0, recv.at[0], (2 * x, o))
 
@@ -269,7 +272,7 @@
     @pl.when(core == 1)
     def _():
         for c in range(2):
-            remote_at(rising, risen.at[c], 55, recv.at[111 + c], (s, up)).wait_recv()
+            remote_at(rising, risen.at[c], 55, recv.at[84 + c], (s, up)).wait_recv()
         pattern[...] = jnp.where(half_mine == 0, risen[0], risen[1])
 
     def misfit(rows, i):
@@ -451,21 +454,18 @@
 
     by_rows(add_pair)
     deep = N // NY
-    y_copies = []
     for k in range(1, NY):
         y_to = rem(y + k, NY)
         rows_to = pl.ds(pl.multiple_of(y_to * deep, deep), deep)
         copy = remote_at(
-            ysend.at[:, rows_to, :], yrecv.at[k - 1], q_y + k - 43, recv.at[q_y + k - 1], (s, y_to * NZ + z)
+            ysend.at[:, rows_to, :], yrecv.at[k - 1], q_y + k - 43, recv.at[79], (s, y_to * NZ + z)
         )
         start(copy)
-        y_copies.append(copy)
     pass_on(0)
     launch(2)
     pass_on(1)
     launch(3)
-    for copy in y_copies:
-        copy.wait_recv()
+    await_all(yrecv, 79)
     rows_me = pl.ds(pl.multiple_of(y * deep, deep), deep)
     totals = []
     for part in range(2):
@@ -475,36 +475,30 @@
         totals.append(total)
     for k in range(NZ):
         zsend[k] = jnp.concatenate([total[8 * k : 8 * k + 8] for total in totals], axis=0).astype(BF)
-    z_copies = []
     for k in range(1, NZ):
         z_to = rem(z + k, NZ)
         copy = remote_at(
-            zsend.at[z_to], zrecv.at[k - 1], q_z + k - 43, recv.at[q_z + k - 1], (s, y * NZ + z_to)
+            zsend.at[z_to], zrecv.at[k - 1], q_z + k - 43, recv.at[80], (s, y * NZ + z_to)
         )
         start(copy)
-        z_copies.append(copy)
     collect(0)
     pass_on(2)
     launch(4)
     collect(1)
     pass_on(3)
-    for copy in z_copies:
-        copy.wait_recv()
+    await_all(zrecv, 80)
     total = zsend[z].astype(F32)
     for k in range(NZ - 1):
         total = total + zrecv[k].astype(F32)
     xall[0] = total.astype(BF)
-    x_copies = []
     for k in range(1, NS):
-        copy = remote_at(xall.at[0], xall.at[k], q_x + k - 43, recv.at[q_x + k - 1], (rem(s + k, NS), o))
+        copy = remote_at(xall.at[0], xall.at[k], q_x + k - 43, recv.at[81], (rem(s + k, NS), o))
         start(copy)
-        x_copies.append(copy)
     collect(2)
     pass_on(4)
     collect(3)
     collect(4)
-    for copy in x_copies:
-        copy.wait_recv()
+    await_all(xall.at[pl.ds(1, NS - 1)], 81)
     pick = one_hot((N, 128), lambda a, b: a == b + 32 * s)
     factor = 1.0 / math.sqrt(256.0)
     shares = [dot(xall[k], pick) for k in range(NS)]
@@ -590,7 +584,7 @@
             vmem((NS, 16, N), BF),
             pltpu.SemaphoreType.DMA((11 + 2 * NS,)),
             pltpu.SemaphoreType.DMA((56,)),
-            pltpu.SemaphoreType.DMA((117,)),
+            pltpu.SemaphoreType.DMA((90,)),
         ],
         compiler_params=pltpu.CompilerParams(
             collective_id=0, has_side_effects=True, vmem_limit_bytes=44 * 1024 * 1024

time: 58.2 us -> 58 us (level)
  no operation moved by 1% of the time
where the time goes in v11:
time: 58 us; the launch traced here: 57.9 us
  Pallas kernels  56.6 us (98%)
  between operations  1.29 us (2%)
    pallas_call x1, Pallas kernels, body(): pl.pallas_call(main_kernel, out_shape=(jax.ShapeDtypeStruct(square(2, 2),...  55.6 us

profile of v11, /device:TPU:1, one launch (start us, length us, event | category | flops | bytes accessed | tf_op | source)
XLA Modules:
  0.0 57.9 jit_solution(2406026072874891081)
XLA Ops:
  1.3 55.6 %gradient.1 = (f32[2,2,256,256]{3,2,1,0:T(8,128)S(1)}, f32[2,2,8,32]{3,2,1,0:T(8,128)S(1)}) custom-call(s32[1,1]{1,0:T(1,128)S(6)} %copy.8.count_ref, s32[2,2]{1,0:T(2,128)} %bitcast.3, f32[2,2,256,2048]{3,2,1,0:T(8,128)} %tile_hbm.1, f32[2,2,256,256]{3,2,1,0:T(8,128)} %probe_hbm.1, bf16[2,256,256]{2,1,0:T(8,128)(2,1)} %bitcast.2, ...), custom_call_target="tpu_custom_call" | custom-call | tf_op jit(solution)/shard_map/gradient/pallas_call | solution.py:541
  56.9 1.0 %results.1 = (f32[2,2,256,256]{3,2,1,0:T(8,128)}, f32[2,2,8,32]{3,2,1,0:T(8,128)}) custom-call(f32[2,2,256,256]{3,2,1,0:T(8,128)S(1)} %get-tuple-element.4.grad_ref, f32[2,2,8,32]{3,2,1,0:T(8,128)S(1)} %get-tuple-element.5.probe_ref), custom_call_target="tpu_custom_call" | custom-call | tf_op jit(solution)/shard_map/results/pallas_call | solution.py:594
